TPU v7x, 32 devices: a whole 2x2x4 slice. The times are simulated.
32 devices in a mesh: seq: 2 (over core), ctx: 8 (over z, x), wt: 2 (over y).
Axes of the slice: x: 2, y: 2, z: 4, core: 2. Of those that a mesh axis runs over, the one named last changes fastest.
Arguments:
- layer_input: bfloat16 [2, 1024, 576], P('seq', 'ctx', 'wt'), may hold values from -32 to 32
- cotangent: bfloat16 [2, 1024, 576], P('seq', 'ctx', 'wt'), may hold values from -6 to 6
- w_qkv: bfloat16 [576, 960], P('wt'), may hold values from -0.25 to 0.25
- w_out: bfloat16 [576, 576], P(None, 'wt'), may hold values from -1.5 to 1.5
- w_gate: bfloat16 [576, 1536], P(None, 'wt'), may hold values from -0.25 to 0.25
- w_up: bfloat16 [576, 1536], P(None, 'wt'), may hold values from -0.25 to 0.25
- w_down: bfloat16 [1536, 576], P('wt'), may hold values from -0.3125 to 0.3125
- gain_attn: float32 [576], P('wt'), may hold values from 0.1 to 1.9
- gain_mlp: float32 [576], P('wt'), may hold values from 0.1 to 1.9
Outputs:
- layer_output: bfloat16 [2, 1024, 576], P('seq', 'ctx', 'wt')
- input_grad: float32 [2, 1024, 576], P('seq', 'ctx', 'wt')
- grad_qkv: float32 [576, 960], P('wt')
- grad_out: float32 [576, 576], P(None, 'wt')
- grad_gate: float32 [576, 1536], P(None, 'wt')
- grad_up: float32 [576, 1536], P(None, 'wt')
- grad_down: float32 [1536, 576], P('wt')
- grad_gain_attn: float32 [576], P('wt')
- grad_gain_mlp: float32 [576], P('wt')
All inputs are finite; a program needn't handle non-finite values.
Results may differ from a plain program's by a relative error of at most 0.04.
Values may be sent and summed in bfloat16 or wider, within the bound.
No kernel may reach another device: no remote copies, remote signals or barrier semaphores. Data moves between devices by JAX's collectives and lax.ppermute only.
A program may use at most 128 MiB of HBM per device.

v0:
```python
import jax
import jax.numpy as jnp
from jax import lax
from jax.sharding import PartitionSpec as P

QUERY_HEADS = 9
KEY_VALUE_HEADS = 3
HEAD_SIZE = 64


EPSILON = 1e-05
ROPE_BASE = 100000.0


def row_sums(partial_value):
    return lax.psum(partial_value, "wt")


def rope_tables(positions):
    half_dim = HEAD_SIZE // 2
    frequency = jnp.power(
        jnp.float32(ROPE_BASE), -jnp.arange(half_dim, dtype=jnp.float32) * 2.0 / HEAD_SIZE
    )
    angles = positions.astype(jnp.float32)[:, None] * frequency[None, :]
    angles = jnp.concatenate([angles, angles], axis=1)
    return (jnp.cos(angles), jnp.sin(angles))


def rotate(tensor):
    half_dim = tensor.shape[-1] // 2
    return jnp.concatenate([-tensor[..., half_dim:], tensor[..., :half_dim]], axis=-1)


def apply_rotation(tensor, cosine_values, sine_values):
    return tensor * cosine_values[:, None, :] + rotate(tensor) * sine_values[:, None, :]


def reverse_rotation(tensor, cosine_values, sine_values):
    return tensor * cosine_values[:, None, :] - rotate(tensor) * sine_values[:, None, :]


def select_group(values_in, group_index):
    return lax.dynamic_index_in_dim(values_in, group_index, 0, keepdims=False)


def fetch_block(kv_stack, source, row_start, key_tile):
    key_value_half = kv_stack.shape[2] // 2
    key_value_block = lax.dynamic_slice(
        kv_stack, (source, row_start, 0), (1, key_tile, kv_stack.shape[2])
    )[0]
    key_portion = key_value_block[:, :key_value_half].reshape(key_tile, KEY_VALUE_HEADS, HEAD_SIZE)
    value_portion = key_value_block[:, key_value_half:].reshape(
        key_tile, KEY_VALUE_HEADS, HEAD_SIZE
    )
    return (key_portion, value_portion)


def on_device(layer_input, cotangent, w_qkv, w_out, w_gate, w_up, w_down, gain_attn, gain_mlp):
    ctx_count = lax.axis_size("ctx")
    wt_count = lax.axis_size("wt")
    ctx_index = lax.axis_index("ctx")
    wt_index = lax.axis_index("wt")
    resid_in = layer_input[0].astype(jnp.float32)
    tok_rows, part_width = resid_in.shape
    full_width = part_width * wt_count
    local_rows = tok_rows // wt_count
    segment_rows = local_rows // 2
    block_rows = tok_rows // 2
    repeat_factor = QUERY_HEADS // KEY_VALUE_HEADS
    query_total_width = QUERY_HEADS * HEAD_SIZE
    key_value_width = KEY_VALUE_HEADS * HEAD_SIZE
    scale_one = lax.rsqrt(row_sums(jnp.sum(resid_in * resid_in, axis=1)) / full_width + EPSILON)[
        :, None
    ]
    normed_one = resid_in * scale_one
    hidden_one = (normed_one * gain_attn).astype(jnp.bfloat16)
    rows_in = hidden_one
    projected_rows = lax.psum_scatter(
        jnp.dot(rows_in, w_qkv, preferred_element_type=jnp.float32).astype(jnp.bfloat16),
        "wt",
        scatter_dimension=0,
        tiled=True,
    ).astype(jnp.float32)
    offsets = jnp.arange(segment_rows, dtype=jnp.int32)
    early_pos = ctx_index * block_rows + wt_index * segment_rows + offsets
    late_pos = (2 * ctx_count - 1 - ctx_index) * block_rows + wt_index * segment_rows + offsets
    query_pos = jnp.stack([early_pos, late_pos])
    cosine_values, sine_values = rope_tables(query_pos.reshape(local_rows))
    query_rows = apply_rotation(
        projected_rows[:, :query_total_width].reshape(local_rows, QUERY_HEADS, HEAD_SIZE),
        cosine_values,
        sine_values,
    )
    query_rows = query_rows.astype(jnp.bfloat16).reshape(
        2, segment_rows, KEY_VALUE_HEADS, repeat_factor, HEAD_SIZE
    )
    key_row_slice = apply_rotation(
        projected_rows[:, query_total_width : query_total_width + key_value_width].reshape(
            local_rows, KEY_VALUE_HEADS, HEAD_SIZE
        ),
        cosine_values,
        sine_values,
    )
    key_row_slice = key_row_slice.astype(jnp.bfloat16).reshape(local_rows, key_value_width)
    value_row_slice = projected_rows[:, query_total_width + key_value_width :].astype(jnp.bfloat16)
    kv_pair = jnp.concatenate([key_row_slice, value_row_slice], axis=1).reshape(
        2, segment_rows, 2 * key_value_width
    )
    kv_all = lax.all_gather(kv_pair, ("ctx", "wt"), axis=1, tiled=True)
    half_len = kv_all.shape[1]
    key_tile = min(1024, half_len)
    block_total = half_len // key_tile
    early_count = (ctx_index * block_rows + (wt_index + 1) * segment_rows - 1) // key_tile + 1
    late_count = (
        (ctx_count - 1 - ctx_index) * block_rows + (wt_index + 1) * segment_rows - 1
    ) // key_tile + 1
    turn_total = early_count + block_total + late_count

    def locate(turn_index):
        query_group = (turn_index >= early_count).astype(jnp.int32)
        late_turn = turn_index - early_count
        source = query_group * (late_turn >= block_total).astype(jnp.int32)
        block_index = jnp.where(
            query_group == 0,
            turn_index,
            jnp.where(source == 0, late_turn, 2 * block_total - 1 - late_turn),
        )
        row_start = block_index * key_tile
        key_index = row_start + jnp.arange(key_tile, dtype=jnp.int32)
        late_keys = (
            2 * ctx_count - 1 - key_index // block_rows
        ) * block_rows + key_index % block_rows
        key_pos = jnp.where(source == 0, key_index, late_keys)
        return (query_group, source, row_start, key_pos)

    def group_scores(kv_stack, turn_index):
        query_group, source, row_start, key_pos = locate(turn_index)
        key_portion, value_portion = fetch_block(kv_stack, source, row_start, key_tile)
        query_sel = select_group(query_rows, query_group)
        scores = (
            jnp.einsum("pgrd,kgd->pgrk", query_sel, key_portion, preferred_element_type=jnp.float32)
            * 0.125
        )
        key_mask = (key_pos[None, :] <= select_group(query_pos, query_group)[:, None])[
            :, None, None, :
        ]
        scores = jnp.where(key_mask, scores, -1e30)
        return (
            query_group,
            source,
            row_start,
            query_sel,
            key_portion,
            value_portion,
            scores,
            key_mask,
        )

    def forward_turn(turn_index, loop_state):
        running_max, running_sum, attended_acc = loop_state
        query_group, source, row_start, query_sel, key_portion, value_portion, scores, key_mask = (
            group_scores(kv_all, turn_index)
        )
        previous = select_group(running_max, query_group)
        updated = jnp.maximum(previous, jnp.max(scores, axis=-1))
        shrink = jnp.exp(previous - updated)
        weights = jnp.where(key_mask, jnp.exp(scores - updated[..., None]), 0.0)
        summed_exp = select_group(running_sum, query_group) * shrink + jnp.sum(weights, axis=-1)
        gained = select_group(attended_acc, query_group) * shrink[..., None] + jnp.einsum(
            "pgrk,kgd->pgrd",
            weights.astype(jnp.bfloat16),
            value_portion,
            preferred_element_type=jnp.float32,
        )
        return (
            lax.dynamic_update_index_in_dim(running_max, updated, query_group, 0),
            lax.dynamic_update_index_in_dim(running_sum, summed_exp, query_group, 0),
            lax.dynamic_update_index_in_dim(attended_acc, gained, query_group, 0),
        )

    statistic_shape = (2, segment_rows, KEY_VALUE_HEADS, repeat_factor)
    running_max, running_sum, attended_acc = lax.fori_loop(
        0,
        turn_total,
        forward_turn,
        (
            jnp.full(statistic_shape, -1e30, jnp.float32),
            jnp.zeros(statistic_shape, jnp.float32),
            jnp.zeros((2, segment_rows, KEY_VALUE_HEADS, repeat_factor, HEAD_SIZE), jnp.float32),
        ),
    )
    logsumexp_every = running_max + jnp.log(running_sum)
    attended_rows = (attended_acc / running_sum[..., None]).astype(jnp.bfloat16)
    attended_all = lax.all_gather(
        attended_rows.reshape(local_rows, query_total_width), "wt", axis=0, tiled=True
    )
    resid_mid = resid_in + jnp.dot(attended_all, w_out, preferred_element_type=jnp.float32)
    scale_two = lax.rsqrt(row_sums(jnp.sum(resid_mid * resid_mid, axis=1)) / full_width + EPSILON)[
        :, None
    ]
    normed_two = resid_mid * scale_two
    hidden_two = (normed_two * gain_mlp).astype(jnp.bfloat16)
    hidden_full = lax.all_gather(hidden_two, "wt", axis=1, tiled=True)
    gate_pre = jnp.dot(hidden_full, w_gate, preferred_element_type=jnp.float32)
    up_pre = jnp.dot(hidden_full, w_up, preferred_element_type=jnp.float32)
    sigmoid_gate = jax.nn.sigmoid(gate_pre)
    activated = (gate_pre * sigmoid_gate * up_pre).astype(jnp.bfloat16)
    down_terms = jnp.dot(activated, w_down, preferred_element_type=jnp.float32)
    mlp_delta = lax.psum_scatter(
        down_terms.astype(jnp.bfloat16), "wt", scatter_dimension=1, tiled=True
    ).astype(jnp.float32)
    layer_out = (resid_mid + mlp_delta).astype(jnp.bfloat16)
    cot_rows = cotangent[0]
    cot_full = lax.all_gather(cot_rows, "wt", axis=1, tiled=True)
    act_grad = jnp.dot(cot_full, w_down.T, preferred_element_type=jnp.float32)
    gate_grad = (act_grad * up_pre * sigmoid_gate * (1.0 + gate_pre * (1.0 - sigmoid_gate))).astype(
        jnp.bfloat16
    )
    up_grad = (act_grad * gate_pre * sigmoid_gate).astype(jnp.bfloat16)
    grad_down = jnp.dot(activated.T, cot_full, preferred_element_type=jnp.float32)
    grad_gate = jnp.dot(hidden_full.T, gate_grad, preferred_element_type=jnp.float32)
    grad_up = jnp.dot(hidden_full.T, up_grad, preferred_element_type=jnp.float32)
    hidden_terms = jnp.dot(gate_grad, w_gate.T, preferred_element_type=jnp.float32) + jnp.dot(
        up_grad, w_up.T, preferred_element_type=jnp.float32
    )
    hidden_two_grad = lax.psum_scatter(
        hidden_terms.astype(jnp.bfloat16), "wt", scatter_dimension=1, tiled=True
    ).astype(jnp.float32)
    grad_gain_mlp = jnp.sum(hidden_two_grad * normed_two, axis=0)
    norm_two_grad = hidden_two_grad * gain_mlp
    mean_two = row_sums(jnp.sum(norm_two_grad * normed_two, axis=1)) / full_width
    mid_grad = cot_rows.astype(jnp.float32) + scale_two * (
        norm_two_grad - normed_two * mean_two[:, None]
    )
    mid_rounded = mid_grad.astype(jnp.bfloat16)
    grad_out = jnp.dot(attended_all.T, mid_rounded, preferred_element_type=jnp.float32)
    rows_in = mid_rounded
    attended_gradient = lax.psum_scatter(
        jnp.dot(rows_in, w_out.T, preferred_element_type=jnp.float32).astype(jnp.bfloat16),
        "wt",
        scatter_dimension=0,
        tiled=True,
    )
    attended_gradient = attended_gradient.reshape(
        2, segment_rows, KEY_VALUE_HEADS, repeat_factor, HEAD_SIZE
    )
    row_delta = jnp.sum(
        attended_gradient.astype(jnp.float32) * attended_rows.astype(jnp.float32), axis=-1
    )
    kv_reused = lax.all_gather(kv_pair, ("ctx", "wt"), axis=1, tiled=True)

    def back_turn(turn_index, loop_state):
        query_acc, kv_acc = loop_state
        query_group, source, row_start, query_sel, key_portion, value_portion, scores, key_mask = (
            group_scores(kv_reused, turn_index)
        )
        grad_sel = select_group(attended_gradient, query_group)
        probs_full = jnp.exp(scores - select_group(logsumexp_every, query_group)[..., None])
        prob_grad = jnp.einsum(
            "pgrd,kgd->pgrk", grad_sel, value_portion, preferred_element_type=jnp.float32
        )
        score_grad = (
            probs_full * (prob_grad - select_group(row_delta, query_group)[..., None])
        ).astype(jnp.bfloat16)
        weight_bf = probs_full.astype(jnp.bfloat16)
        query_new = (
            select_group(query_acc, query_group)
            + jnp.einsum(
                "pgrk,kgd->pgrd", score_grad, key_portion, preferred_element_type=jnp.float32
            )
            * 0.125
        )
        key_part_grad = (
            jnp.einsum("pgrk,pgrd->kgd", score_grad, query_sel, preferred_element_type=jnp.float32)
            * 0.125
        )
        value_part_grad = jnp.einsum(
            "pgrk,pgrd->kgd", weight_bf, grad_sel, preferred_element_type=jnp.float32
        )
        update_rows = jnp.concatenate(
            [
                key_part_grad.reshape(key_tile, key_value_width),
                value_part_grad.reshape(key_tile, key_value_width),
            ],
            axis=1,
        )[None]
        previous = lax.dynamic_slice(kv_acc, (source, row_start, 0), update_rows.shape)
        kv_acc = lax.dynamic_update_slice(kv_acc, previous + update_rows, (source, row_start, 0))
        return (lax.dynamic_update_index_in_dim(query_acc, query_new, query_group, 0), kv_acc)

    query_acc, kv_acc = lax.fori_loop(
        0,
        turn_total,
        back_turn,
        (
            jnp.zeros((2, segment_rows, KEY_VALUE_HEADS, repeat_factor, HEAD_SIZE), jnp.float32),
            jnp.zeros((2, half_len, 2 * key_value_width), jnp.float32),
        ),
    )
    key_value_gradient = lax.psum_scatter(
        kv_acc, ("ctx", "wt"), scatter_dimension=1, tiled=True
    ).reshape(local_rows, 2 * key_value_width)
    query_gradient = reverse_rotation(
        query_acc.reshape(local_rows, QUERY_HEADS, HEAD_SIZE), cosine_values, sine_values
    )
    key_gradient = reverse_rotation(
        key_value_gradient[:, :key_value_width].reshape(local_rows, KEY_VALUE_HEADS, HEAD_SIZE),
        cosine_values,
        sine_values,
    )
    proj_grad = jnp.concatenate(
        [
            query_gradient.reshape(local_rows, query_total_width),
            key_gradient.reshape(local_rows, key_value_width),
            key_value_gradient[:, key_value_width:],
        ],
        axis=1,
    ).astype(jnp.bfloat16)
    proj_all = lax.all_gather(proj_grad, "wt", axis=0, tiled=True)
    grad_qkv = jnp.dot(hidden_one.T, proj_all, preferred_element_type=jnp.float32)
    hidden_one_grad = jnp.dot(proj_all, w_qkv.T, preferred_element_type=jnp.float32)
    grad_gain_attn = jnp.sum(hidden_one_grad * normed_one, axis=0)
    norm_one_grad = hidden_one_grad * gain_attn
    mean_one = row_sums(jnp.sum(norm_one_grad * normed_one, axis=1)) / full_width
    input_grad = mid_grad + scale_one * (norm_one_grad - normed_one * mean_one[:, None])
    summed = lax.psum(
        (grad_qkv, grad_out, grad_gate, grad_up, grad_down, grad_gain_attn, grad_gain_mlp),
        ("seq", "ctx"),
    )
    return (
        layer_out[None],
        input_grad[None],
        summed[0],
        summed[1],
        summed[2],
        summed[3],
        summed[4],
        summed[5],
        summed[6],
    )


def solution(mesh):
    in_specs = (
        P("seq", "ctx", "wt"),
        P("seq", "ctx", "wt"),
        P("wt", None),
        P(None, "wt"),
        P(None, "wt"),
        P(None, "wt"),
        P("wt", None),
        P("wt"),
        P("wt"),
    )
    out_specs = (
        P("seq", "ctx", "wt"),
        P("seq", "ctx", "wt"),
        P("wt", None),
        P(None, "wt"),
        P(None, "wt"),
        P(None, "wt"),
        P("wt", None),
        P("wt"),
        P("wt"),
    )
    return jax.shard_map(
        on_device, mesh=mesh, in_specs=in_specs, out_specs=out_specs, check_vma=False
    )
```

profile of v0, /device:TPU:0, one launch (start us, length us, event | category | flops | bytes accessed | tf_op | source)
XLA Modules:
  0.0 496.8 jit_solution(12847941043045343136)
XLA Ops:
  8.3 5.9 %psum.77 = f32[128]{0:T(128)S(1)} all-reduce(f32[128]{0:T(128)S(1)} %fusion.80), channel_id=1, replica_groups=mesh['seq'=2,'ctx'=8,'wt'=2] {'wt'}, use_global_device_ids=true, to_apply=%region_1.0 | all-reduce | flops 128 | bytes 1024 | tf_op jit(solution)/shard_map/psum | solution.py:16
  14.7 2.3 convolution_convert_fusion
  18.6 5.1 %all-gather = bf16[1,128,576]{1,2,0:T(8,128)(2,1)} all-gather(bf16[1,128,288]{1,2,0:T(8,128)(2,1)S(1)} %copy-done.34), channel_id=2, replica_groups=mesh['seq'=2,'ctx'=8,'wt'=2] {'wt'}, dimensions={2}, use_global_device_ids=true | all-gather | bytes 221184 | tf_op jit(solution)/shard_map/all_gather | solution.py:214
  24.0 6.6 %reduce-scatter.6.cloned.1.call-done = bf16[64,960]{1,0:T(8,128)(2,1)} async-done(((bf16[128,960]{1,0:T(8,128)(2,1)}), bf16[64,960]{1,0:T(8,128)(2,1)}) %reduce-scatter.6.cloned.1.call-update) | async-done | bytes 122896 | tf_op jit(solution)/shard_map/reduce_scatter | solution.py:78
  35.2 44.6 %all_gather.16 = bf16[2,512,384]{2,0,1:T(2,128)(2,1)S(1)} all-gather(bf16[2,32,384]{2,0,1:T(2,128)(2,1)S(1)} %copy.71), channel_id=1, replica_groups=mesh['seq'=2,'ctx'=8,'wt'=2] {'ctx','wt'}, dimensions={1}, use_global_device_ids=true | all-gather | bytes 835584 | tf_op jit(solution)/shard_map/all_gather | solution.py:109
  79.8 2.1 copy.75
  82.0 11.2 %while.30 = (s32[]{:T(128)}, f32[2,32,3,3]{1,3,2,0:T(4,128)S(1)}, f32[2,32,3,3]{1,3,2,0:T(4,128)S(1)}, f32[2,32,3,3,64]{4,1,3,2,0:T(8,128)S(1)}, s32[]{:T(128)},...) while((s32[]{:T(128)}, f32[2,32,3,3]{1,3,2,0:T(4,128)S(1)}, ...), condition=%wide.region_6.7_spmd, body=%wide.region_3.6_spmd.sunk | while | flops 39142544 | bytes 4379230 | solution.py:182
  83.9 1.2 fusion.173
  87.7 1.2 fusion.173
  91.4 1.2 fusion.173
  94.4 1.7 reshape.372
  96.1 5.4 %all_gather.17 = bf16[128,576]{1,0:T(8,128)(2,1)S(1)} all-gather(bf16[64,576]{1,0:T(8,128)(2,1)} %reshape.372), channel_id=1, replica_groups=mesh['seq'=2,'ctx'=8,'wt'=2] {'wt'}, dimensions={0}, use_global_device_ids=true | all-gather | bytes 221184 | tf_op jit(solution)/shard_map/all_gather | solution.py:194
  102.4 5.0 %psum.78 = f32[128]{0:T(128)S(1)} all-reduce(f32[128]{0:T(128)} %get-tuple-element.432), channel_id=1, replica_groups=mesh['seq'=2,'ctx'=8,'wt'=2] {'wt'}, use_global_device_ids=true, to_apply=%region_8.9 | all-reduce | flops 128 | bytes 1024 | tf_op jit(solution)/shard_map/psum | solution.py:16
  107.9 5.0 %all_gather.18 = bf16[128,576]{0,1:T(8,128)(2,1)S(1)} all-gather(bf16[128,288]{0,1:T(8,128)(2,1)S(1)} %multiply_convert_fusion.3), channel_id=1, replica_groups=mesh['seq'=2,'ctx'=8,'wt'=2] {'wt'}, dimensions={1}, use_global_device_ids=true | all-gather | bytes 221184 | tf_op jit(solution)/shard_map/all_gather | solution.py:203
  117.9 5.4 %reduce-scatter.10.cloned.1.call-done = bf16[128,288]{0,1:T(8,128)(2,1)} async-done(((bf16[128,576]{0,1:T(8,128)(2,1)}), bf16[128,288]{0,1:T(8,128)(2,1)}) %reduce-scatter.10.cloned.1.call-update) | async-done | bytes 73744 | tf_op jit(solution)/shard_map/reduce_scatter | solution.py:226
  123.3 1.7 fusion.72
  124.9 4.9 psum.79
  129.8 6.8 %reduce-scatter.8.cloned.1.call-done = bf16[128,288]{0,1:T(8,128)(2,1)} async-done(((bf16[128,576]{0,1:T(8,128)(2,1)}), bf16[128,288]{0,1:T(8,128)(2,1)}) %reduce-scatter.8.cloned.1.call-update) | async-done | bytes 73744 | tf_op jit(solution)/shard_map/reduce_scatter | solution.py:209
  136.6 1.6 fusion.71
  139.8 10.1 %reduce-scatter.12.cloned.1.call-done = bf16[64,576]{1,0:T(8,128)(2,1)} async-done(((bf16[128,576]{1,0:T(8,128)(2,1)}), bf16[64,576]{1,0:T(8,128)(2,1)}) %reduce-scatter.12.cloned.1.call-update) | async-done | bytes 73744 | tf_op jit(solution)/shard_map/reduce_scatter | solution.py:238
  152.5 1.3 broadcast_in_dim.112.clone
  153.8 38.4 %while.31 = (s32[]{:T(128)}, f32[2,32,3,3,64]{4,1,3,2,0:T(8,128)S(1)}, f32[2,512,384]{2,1,0:T(8,128)}, s32[]{:T(128)}, s32[]{:T(128)}, /*index=5*/bf16[2,512,384...) while((s32[]{:T(128)}, ...), condition=%wide.region_16.17_spmd, body=%wide.region_15.16_spmd.sunk | while | flops 95961104 | bytes 15035902 | solution.py:291
  156.3 1.1 fusion.191
  158.6 1.9 fusion.194
  160.7 1.9 fusion.195
  162.6 1.2 constant_dynamic-slice_fusion.10
  164.1 1.3 fusion.196
  171.4 1.9 fusion.194
  173.5 1.9 fusion.195
  175.4 1.2 constant_dynamic-slice_fusion.10
  176.9 1.3 fusion.196
  184.2 1.9 fusion.194
  186.3 1.9 fusion.195
  188.2 1.2 constant_dynamic-slice_fusion.10
  189.7 1.3 fusion.196
  194.3 1.6 fusion.81
  195.9 1.6 fusion.105
  197.5 1.6 fusion.104
  201.3 117.1 %reduce-scatter.14.cloned.1.call-done = f32[2,32,384]{2,1,0:T(8,128)} async-done(((f32[2,512,384]{2,1,0:T(8,128)}), f32[2,32,384]{2,1,0:T(8,128)}) %reduce-scatter.14.cloned.1.call-update) | async-done | bytes 98320 | tf_op jit(solution)/shard_map/reduce_scatter | solution.py:300
  320.6 5.6 %all_gather.20 = bf16[128,960]{1,0:T(8,128)(2,1)S(1)} all-gather(bf16[64,960]{1,0:T(8,128)(2,1)S(1)} %pad_maximum_fusion), channel_id=1, replica_groups=mesh['seq'=2,'ctx'=8,'wt'=2] {'wt'}, dimensions={0}, use_global_device_ids=true | all-gather | bytes 368640 | tf_op jit(solution)/shard_map/all_gather | solution.py:319
  326.3 1.4 fusion.94
  329.1 4.9 psum.80
  334.1 33.2 %all-reduce = (f32[288]{0:T(512)}, f32[288]{0:T(512)}) all-reduce(f32[288]{0:T(512)S(1)} %get-tuple-element.352, f32[288]{0:T(512)S(1)} %copy-done.40), channel_id=1, replica_groups=mesh['seq'=2,'ctx'=8,'wt'=2] {'seq','ctx'}, use_global_device_ids=true, to_apply=%region_26.27 | all-reduce | flops 576 | bytes 4608 | tf_op jit(solution)/shard_map/psum | solution.py:326
  368.0 113.1 %all-reduce.4.cloned.1.call-done = (f32[288,960]{1,0:T(8,128)}, f32[576,288]{0,1:T(8,128)}, f32[576,768]{1,0:T(8,128)}, f32[576,768]{1,0:T(8,128)}, f32[768,576]{0,1:T(8,128)}) async-done(((f32[288,960]{1,0:T(8,128)}, f32[576,288]{0,1:T(8,128)}, f32[576,768]{1,0:T(8,128)}, f32[576,768]{1,0:T(8,128)}, f32[768,576]{0,1:T(8,128)}), (f32[288,960]{1,0:T(8,128)}, f32[576,288]{0,1:T(8,128)}, f32[576,768]{1,0:T(8,128)}, ...) | async-done | bytes 7077904 | tf_op jit(solution)/shard_map/psum | solution.py:326
  481.1 2.6 copy.149
  484.5 1.2 copy.151
  486.6 1.2 copy.152
  488.8 1.2 copy.153
  (245 shorter events, 56.4 us)
Async XLA Ops:
  7.2 106.5 %copy-start = (bf16[768,576]{0,1:T(8,128)(2,1)S(1)}, bf16[768,576]{0,1:T(8,128)(2,1)}, u32[]{:S(2)}) copy-start(bf16[768,576]{0,1:T(8,128)(2,1)} %param.19) | copy-start | bytes 2654212
  7.2 11.4 %copy-start.34 = (bf16[1,128,288]{1,2,0:T(8,128)(2,1)S(1)}, bf16[1,128,288]{1,2,0:T(8,128)(2,1)}, u32[]{:S(2)}) copy-start(bf16[1,128,288]{1,2,0:T(8,128)(2,1)} %param.14) | copy-start | bytes 221188
  7.2 23.4 %reduce-scatter.6.cloned.1.call-start = ((), (), s32[]{:S(2)}) async-start(), calls=%async_computation.5 | async-start | bytes 393216 | tf_op jit(solution)/shard_map/reduce_scatter | solution.py:78
  17.0 106.3 %reduce-scatter.10.cloned.1.call-start = ((), (), s32[]{:S(2)}) async-start(), calls=%async_computation.7 | async-start | bytes 221184 | tf_op jit(solution)/shard_map/reduce_scatter | solution.py:226
  17.9 0.6 copy-start.30
  17.9 15.3 %copy-start.28 = (f32[64,64]{0,1:T(8,128)}, f32[64,64]{0,1:T(8,128)S(1)}, u32[]{:S(2)}) copy-start(f32[64,64]{0,1:T(8,128)S(1)} %get-tuple-element.429) | copy-start | bytes 49156
  30.6 2.4 copy-start.16
  30.7 2.6 slice-start
  81.9 19.6 %copy-start.5 = (bf16[1,128,288]{1,2,0:T(8,128)(2,1)S(1)}, bf16[1,128,288]{1,2,0:T(8,128)(2,1)}, u32[]{:S(2)}) copy-start(bf16[1,128,288]{1,2,0:T(8,128)(2,1)} %param.13) | copy-start | bytes 221188
  82.0 19.6 %copy-start.13 = (bf16[576,288]{0,1:T(8,128)(2,1)S(1)}, bf16[576,288]{0,1:T(8,128)(2,1)}, u32[]{:S(2)}) copy-start(bf16[576,288]{0,1:T(8,128)(2,1)} %param.16) | copy-start | bytes 995332
  93.2 2.9 copy-start.32
  93.2 14.2 %copy-start.37 = (f32[288]{0:T(512)S(1)}, f32[288]{0:T(512)}, u32[]{:S(2)}) copy-start(f32[288]{0:T(512)} %param.21) | copy-start | bytes 3460
  93.2 19.7 %copy-start.4 = (bf16[576,768]{1,0:T(8,128)(2,1)S(1)}, bf16[576,768]{1,0:T(8,128)(2,1)}, u32[]{:S(2)}) copy-start(bf16[576,768]{1,0:T(8,128)(2,1)} %param.18) | copy-start | bytes 2654212
  93.4 2.7 copy-start.17
  93.4 19.9 %copy-start.3 = (bf16[576,768]{1,0:T(8,128)(2,1)S(1)}, bf16[576,768]{1,0:T(8,128)(2,1)}, u32[]{:S(2)}) copy-start(bf16[576,768]{1,0:T(8,128)(2,1)} %param.17) | copy-start | bytes 2654212
  101.5 0.8 copy-start.14
  107.4 6.3 %copy-start.26 = (bf16[1,128,576]{1,2,0:T(8,128)(2,1)S(1)}, bf16[1,128,576]{1,2,0:T(8,128)(2,1)}, u32[]{:S(2)}) copy-start(bf16[1,128,576]{1,2,0:T(8,128)(2,1)} %all-gather) | copy-start | bytes 442372
  112.9 1.9 copy-start.1
  114.8 0.7 copy-start.19
  114.8 0.8 copy-start.23
  115.2 1.5 copy-start.21
  115.2 8.0 %copy-start.42 = (f32[128]{0:T(128)S(1)}, f32[128]{0:T(128)}, u32[]{:S(2)}) copy-start(f32[128]{0:T(128)} %copy-done.41) | copy-start | bytes 1540
  115.3 21.3 %copy-start.35 = (bf16[1,128,288]{1,2,0:T(8,128)(2,1)S(1)}, bf16[1,128,288]{1,2,0:T(8,128)(2,1)}, u32[]{:S(2)}) copy-start(bf16[1,128,288]{1,2,0:T(8,128)(2,1)} %param.14) | copy-start | bytes 221188
  116.7 22.5 %copy-start.33 = (f32[2,32,3,3]{1,3,2,0:T(4,128)S(1)}, f32[2,32,3,3]{1,3,2,0:T(4,128)}, u32[]{:S(2)}) copy-start(f32[2,32,3,3]{1,3,2,0:T(4,128)} %copy-done.32) | copy-start | bytes 6916
  116.7 34.4 %copy-start.18 = (f32[2,32,3,3]{3,2,1,0:T(4,128)S(1)}, f32[2,32,3,3]{3,2,1,0:T(4,128)}, u32[]{:S(2)}) copy-start(f32[2,32,3,3]{3,2,1,0:T(4,128)} %copy-done.17) | copy-start | bytes 6916
  116.7 19.9 %reduce-scatter.8.cloned.1.call-start = ((), (), s32[]{:S(2)}) async-start(), calls=%async_computation.6 | async-start | bytes 221184 | tf_op jit(solution)/shard_map/reduce_scatter | solution.py:209
  117.8 32.1 %reduce-scatter.12.cloned.1.call-start = ((), (), s32[]{:S(2)}) async-start(), calls=%async_computation.8 | async-start | bytes 245760 | tf_op jit(solution)/shard_map/reduce_scatter | solution.py:238
  138.2 15.6 %copy-start.8 = (f32[128,288]{0,1:T(8,128)}, f32[128,288]{0,1:T(8,128)S(1)}, u32[]{:S(2)}) copy-start(f32[128,288]{0,1:T(8,128)S(1)} %get-tuple-element.420) | copy-start | bytes 442372
  139.2 179.3 %reduce-scatter.14.cloned.1.call-start = ((), (), s32[]{:S(2)}) async-start(), calls=%async_computation.9 | async-start | bytes 1671168 | tf_op jit(solution)/shard_map/reduce_scatter | solution.py:300
  192.2 2.1 copy-start.22
  192.2 2.1 copy-start.27
  192.2 3.7 copy-start.2
  192.2 3.7 copy-start.20
  192.2 288.9 %all-reduce.4.cloned.1.call-start = ((), (), s32[]{:S(2)}) async-start(), calls=%async_computation.10 | async-start | bytes 14450688 | tf_op jit(solution)/shard_map/psum | solution.py:326
  194.3 3.2 copy-start.24
  195.9 3.2 copy-start.9
  195.9 3.2 copy-start.15
  200.8 119.6 %copy-start.29 = (f32[64,64]{0,1:T(8,128)S(1)}, f32[64,64]{0,1:T(8,128)}, u32[]{:S(2)}) copy-start(f32[64,64]{0,1:T(8,128)} %copy-done.28) | copy-start | bytes 49156
  200.8 119.6 %copy-start.31 = (f32[64,64]{0,1:T(8,128)S(1)}, f32[64,64]{0,1:T(8,128)}, u32[]{:S(2)}) copy-start(f32[64,64]{0,1:T(8,128)} %copy-done.30) | copy-start | bytes 49156
  201.0 125.3 %copy-start.6 = (bf16[1,128,288]{1,2,0:T(8,128)(2,1)S(1)}, bf16[1,128,288]{1,2,0:T(8,128)(2,1)}, u32[]{:S(2)}) copy-start(bf16[1,128,288]{1,2,0:T(8,128)(2,1)} %param.13) | copy-start | bytes 221188
  201.0 125.3 %copy-start.36 = (f32[288]{0:T(512)S(1)}, f32[288]{0:T(512)}, u32[]{:S(2)}) copy-start(f32[288]{0:T(512)} %param.20) | copy-start | bytes 3460
  201.0 125.3 %copy-start.39 = (f32[128]{0:T(128)S(1)}, f32[128]{0:T(128)}, u32[]{:S(2)}) copy-start(f32[128]{0:T(128)} %copy-done.38) | copy-start | bytes 1540
  327.6 1.1 copy-start.7
  327.6 6.4 %copy-start.40 = (f32[288]{0:T(512)S(1)}, f32[288]{0:T(512)}, u32[]{:S(2)}) copy-start(f32[288]{0:T(512)} %get-tuple-element.350) | copy-start | bytes 3460
  481.1 2.6 copy-start.25
  481.1 3.4 copy-start.12
  484.5 2.1 copy-start.11
  486.6 2.1 copy-start.10
  (2 other events, 1.0 us)
Sparse Core Ops, SparseCore 0:
  17.1 13.5 reduce-scatter.5
  116.8 6.3 reduce-scatter.9
  126.1 10.5 reduce-scatter.7
  139.3 10.6 reduce-scatter.11
  192.3 126.1 reduce-scatter.13
  327.8 153.2 all-reduce.3
where the time goes:
time: 499 us; the launch traced here: 497 us
  waiting for transfers between devices  259 us (52%)
  blocking collectives  120 us (24%)
  local copies, waits for them, and re-layouts  48.3 us (10%)
  matrix products  39.3 us (8%)
  between operations  14.8 us (3%)
  other arithmetic  14.6 us (3%)
    reduce_scatter x1, waiting for transfers between devices, on_device(): lax.psum_scatter(kv_acc, ('ctx', 'wt'), scatter_dimension=1, tiled=True)  117 us
    psum x1, waiting for transfers between devices, on_device(): lax.psum((grad_qkv, grad_out, grad_gate, grad_up, grad_down, grad_gain_at...  113 us
    all_gather x1, blocking collectives, on_device(): kv_all = lax.all_gather(kv_pair, ('ctx', 'wt'), axis=1, tiled=True)  44.6 us
    psum x1, blocking collectives, on_device(): lax.psum((grad_qkv, grad_out, grad_gate, grad_up, grad_down, grad_gain_at...  33.2 us
    psum x4, blocking collectives, row_sums(): return lax.psum(partial_value, 'wt')  20.8 us
    unnamed x92, local copies, waits for them, and re-layouts  12 us
    reduce_scatter x1, waiting for transfers between devices, on_device(): lax.psum_scatter(jnp.dot(rows_in, w_out.T, preferred_element_type=jnp.flo...  10.1 us
  transfers between devices with their start and end apart: 6, of which 6 were waited for; matrix products, arithmetic and copies ran while one was open for 3% of the time, Pallas kernels for 0%

commit v1 on v0

--- a/solution.py
+++ b/solution.py
@@ -1,6 +1,8 @@
 import jax
 import jax.numpy as jnp
 from jax import lax
+from jax.experimental import pallas as pl
+from jax.experimental.pallas import tpu as pltpu
 from jax.sharding import PartitionSpec as P
 
 QUERY_HEADS = 9
@@ -55,7 +57,7 @@
     return (key_portion, value_portion)
 
 
-def on_device(layer_input, cotangent, w_qkv, w_out, w_gate, w_up, w_down, gain_attn, gain_mlp):
+def split_device(layer_input, cotangent, w_qkv, w_out, w_gate, w_up, w_down, gain_attn, gain_mlp):
     ctx_count = lax.axis_size("ctx")
     wt_count = lax.axis_size("wt")
     ctx_index = lax.axis_index("ctx")
@@ -340,6 +342,583 @@
     )
 
 
+FORWARD_TILE = 512
+BACKWARD_TILE = 256
+HIDDEN_TILE = 256
+ROW_DISTANCES = (0, 4, 2, 6)
+NN = (((1,), (0,)), ((), ()))
+NT = (((1,), (1,)), ((), ()))
+TN = (((0,), (0,)), ((), ()))
+BF = jnp.bfloat16
+F32 = jnp.float32
+VMEM = pl.BlockSpec(memory_space=pltpu.VMEM)
+SMEM = pl.BlockSpec(memory_space=pltpu.SMEM)
+ANY = pl.BlockSpec(memory_space=pl.ANY)
+
+
+def swap(value, axis, distance, count):
+    return lax.ppermute(value, axis, [(i, i ^ distance) for i in range(count)])
+
+
+def mul(first, second, dims=NN):
+    return lax.dot_general(first, second, dims, preferred_element_type=F32)
+
+
+def in_order(own, other, index, axis):
+    return jnp.where(
+        index == 0,
+        jnp.concatenate([own, other], axis=axis),
+        jnp.concatenate([other, own], axis=axis),
+    )
+
+
+def my_half(value, wt):
+    half = value.shape[1] // 2
+    return jnp.where(wt == 0, value[:, :half], value[:, half:])
+
+
+def turned(value):
+    return value.astype(F32).T.astype(BF)
+
+
+def store_rows(out, full, owner, last):
+    piece = full.shape[0] // 4
+    for j in range(4):
+        base = owner if j % 2 == 0 else last - owner
+        start = pl.multiple_of(base * (2 * piece) + (j // 2) * piece, piece)
+        out[pl.ds(start, piece), :] = full[j * piece : (j + 1) * piece]
+
+
+def own_rows(ref, ctx, last, tok_rows):
+    piece = tok_rows // 4
+    parts = []
+    for j in range(4):
+        base = ctx if j % 2 == 0 else last - ctx
+        start = pl.multiple_of(base * (2 * piece) + (j // 2) * piece, piece)
+        parts.append(ref[pl.ds(start, piece), :])
+    return jnp.concatenate(parts, axis=0)
+
+
+def rotated(first, second, cosines, sines, sign):
+    return first * cosines - sign * second * sines, second * cosines + sign * first * sines
+
+
+def norm_scale(value):
+    return lax.rsqrt(jnp.mean(value * value, axis=1, keepdims=True) + EPSILON)
+
+
+def forward_kernel(
+    where_ref,
+    rows_ref,
+    near_ref,
+    across_ref,
+    low_ref,
+    high_ref,
+    proj_ref,
+    first_ref,
+    second_ref,
+    gain_ref,
+    other_gain_ref,
+    cos_ref,
+    sin_ref,
+    x_ref,
+    h1_ref,
+    q_ref,
+    k_ref,
+    v_ref,
+    o_ref,
+    lse_ref,
+    resid_ref,
+    h2_ref,
+    h2t_ref,
+    weights_ref,
+    h1t_ref,
+    other_ref,
+):
+    ctx, wt, seq = where_ref[0], where_ref[1], where_ref[2]
+    count, tok_rows, part_width = rows_ref.shape
+    last = 4 * count - 1
+    rows = x_ref.shape[0]
+    query_width = QUERY_HEADS * HEAD_SIZE
+    pair_width = KEY_VALUE_HEADS * HEAD_SIZE
+    half_dim = HEAD_SIZE // 2
+    for k in range(count):
+        for d in range(2):
+            own = rows_ref[k] if d == 0 else near_ref[k]
+            if d == 0:
+                other = across_ref[k]
+            else:
+                other = low_ref[k] if k < count // 2 else high_ref[k - count // 2]
+            owner = jnp.bitwise_xor(ctx, ROW_DISTANCES[k] + d)
+            store_rows(x_ref, in_order(own, other, wt, 1), owner, last)
+    half = first_ref.shape[0]
+    other_ref[pl.ds(pl.multiple_of(seq * half, 16), half), :] = first_ref[...]
+    other_ref[pl.ds(pl.multiple_of((1 - seq) * half, 16), half), :] = second_ref[...]
+    weights_ref[...] = in_order(proj_ref[...], other_ref[...], wt, 1)
+    gains = in_order(gain_ref[...], other_gain_ref[...], wt, 1)
+    x = x_ref[...].astype(F32)
+    hidden_one = x * norm_scale(x) * gains[0:1]
+    h1t_ref[...] = hidden_one.T.astype(BF)
+    h1_ref[...] = h1t_ref[pl.ds(pl.multiple_of(wt * part_width, 16), part_width), :]
+    cosines, sines = cos_ref[...], sin_ref[...]
+    heads = QUERY_HEADS + 2 * KEY_VALUE_HEADS
+    for head in range(heads):
+        at = head * HEAD_SIZE
+        value = mul(weights_ref[at : at + HEAD_SIZE], h1t_ref[...])
+        if at < query_width + pair_width:
+            low, high = rotated(value[:half_dim], value[half_dim:], cosines, sines, 1.0)
+            value = jnp.concatenate([low, high], axis=0)
+        if at < query_width:
+            q_ref[at : at + HEAD_SIZE] = value.astype(BF) * BF(0.125)
+        elif at < query_width + pair_width:
+            at -= query_width
+            k_ref[at : at + HEAD_SIZE] = value.astype(BF)
+        else:
+            at -= query_width + pair_width
+            v_ref[at : at + HEAD_SIZE] = value.astype(BF)
+
+    repeat = QUERY_HEADS // KEY_VALUE_HEADS
+    tile = min(FORWARD_TILE, rows)
+    causal = lax.broadcasted_iota(jnp.int32, (tile, tile), 0) <= lax.broadcasted_iota(
+        jnp.int32, (tile, tile), 1
+    )
+
+    def group(g, carry):
+        pair_at = pl.ds(pl.multiple_of(g * HEAD_SIZE, HEAD_SIZE), HEAD_SIZE)
+        keys = turned(k_ref[pair_at, :])
+        values = jnp.concatenate([v_ref[pair_at, :], jnp.ones((16, rows), BF)], axis=0)
+        for r in range(repeat):
+            head = g * repeat + r
+            head_at = pl.ds(pl.multiple_of(head * HEAD_SIZE, HEAD_SIZE), HEAD_SIZE)
+            for start in range(0, rows, tile):
+                stop = start + tile
+                query = q_ref[head_at, start:stop]
+                scores = jnp.where(causal, mul(keys[start:stop], query), -1e30)
+                top = jnp.max(scores, axis=0, keepdims=True)
+                if start:
+                    before = mul(keys[:start], query)
+                    top = jnp.maximum(top, jnp.max(before, axis=0, keepdims=True))
+                weights = jnp.exp(scores - top).astype(BF)
+                out = mul(values[:, start:stop], weights)
+                if start:
+                    out += mul(values[:, :start], jnp.exp(before - top).astype(BF))
+                total = out[HEAD_SIZE : HEAD_SIZE + 1]
+                o_ref[head_at, start:stop] = (out[:HEAD_SIZE] / total).astype(BF)
+                lse_ref[head, :, start:stop] = top + jnp.log(total)
+        return carry
+
+    lax.fori_loop(0, KEY_VALUE_HEADS, group, 0)
+    out_weights = weights_ref[query_width + 2 * pair_width :]
+    resid = x_ref[...].astype(F32) + mul(o_ref[...], out_weights, TN)
+    resid_ref[...] = resid
+    hidden_two = resid * norm_scale(resid) * gains[1:2]
+    h2_ref[...] = hidden_two.astype(BF)
+    h2t_ref[...] = hidden_two.T.astype(BF)
+
+
+def mlp_chunk(hidden_two, cots, gate, up, down):
+    gate_pre = mul(hidden_two, gate, NT)
+    up_pre = mul(hidden_two, up, NT)
+    act_grad = mul(cots, down, NT)
+    sigmoid_gate = jax.nn.sigmoid(gate_pre)
+    silu = gate_pre * sigmoid_gate
+    activated = (silu * up_pre).astype(BF)
+    gate_grad = (act_grad * up_pre * (sigmoid_gate + silu * (1.0 - sigmoid_gate))).astype(BF)
+    up_grad = (act_grad * silu).astype(BF)
+    back = mul(gate_grad, gate) + mul(up_grad, up)
+    return activated, gate_grad, up_grad, back
+
+
+def own_mlp_kernel(
+    where_ref,
+    pairs_ref,
+    far_ref,
+    h2_ref,
+    h2t_ref,
+    w_ref,
+    cot_ref,
+    grads_ref,
+    grad_down_ref,
+    back_ref,
+    delta_ref,
+    act_ref,
+):
+    ctx, wt = where_ref[0], where_ref[1]
+    count, _, tok_rows, part_width = pairs_ref.shape
+    last = 4 * count - 1
+    for k in range(2 * count):
+        ref = pairs_ref if k < count else far_ref
+        full = in_order(ref[k % count, 0], ref[k % count, 1], wt, 1)
+        store_rows(cot_ref, full, jnp.bitwise_xor(ctx, k), last)
+    hidden = w_ref.shape[1]
+    tile = HIDDEN_TILE
+    back_ref[...] = jnp.zeros_like(back_ref)
+    delta_ref[...] = jnp.zeros_like(delta_ref)
+
+    def chunk(j, carry):
+        at = pl.ds(pl.multiple_of(j * tile, tile), tile)
+        down = w_ref[2, at, :]
+        activated, gate_grad, up_grad, back = mlp_chunk(
+            h2_ref[...], cot_ref[...], w_ref[0, at, :], w_ref[1, at, :], down
+        )
+        back_ref[...] += back
+        act_ref[...] = activated
+        delta_ref[...] += mul(own_rows(act_ref, ctx, last, tok_rows), down)
+        grads_ref[0, :, at] = mul(h2t_ref[...], gate_grad).astype(BF)
+        grads_ref[1, :, at] = mul(h2t_ref[...], up_grad).astype(BF)
+        grad_down_ref[at, :] = mul(activated, cot_ref[...], TN).astype(BF)
+        return carry
+
+    lax.fori_loop(0, hidden // tile, chunk, 0)
+
+
+def other_mlp_kernel(
+    where_ref,
+    h2_ref,
+    cot_ref,
+    first_ref,
+    second_ref,
+    back_in_ref,
+    delta_in_ref,
+    resid_ref,
+    gain_ref,
+    other_gain_ref,
+    o_ref,
+    out_ref,
+    mid_ref,
+    mid_bf_ref,
+    grad_out_ref,
+    w_ref,
+    act_ref,
+    back_ref,
+    delta_ref,
+):
+    ctx, wt = where_ref[0], where_ref[1]
+    rows = h2_ref.shape[0]
+    tok_rows, part_width = out_ref.shape
+    last = 2 * rows // tok_rows - 1
+    half = first_ref.shape[1]
+    w_ref[:, :half] = first_ref[...]
+    w_ref[:, half:] = second_ref[...]
+    tile = HIDDEN_TILE
+    back_ref[...] = back_in_ref[...]
+    delta_ref[...] = delta_in_ref[...]
+
+    def chunk(j, carry):
+        at = pl.ds(pl.multiple_of(j * tile, tile), tile)
+        down = w_ref[2, at, :]
+        activated, _, _, back = mlp_chunk(
+            h2_ref[...], cot_ref[...], w_ref[0, at, :], w_ref[1, at, :], down
+        )
+        back_ref[...] += back
+        act_ref[...] = activated
+        delta_ref[...] += mul(own_rows(act_ref, ctx, last, tok_rows), down)
+        return carry
+
+    lax.fori_loop(0, 2 * half // tile, chunk, 0)
+    gains = in_order(gain_ref[...], other_gain_ref[...], wt, 1)
+    layer_out = own_rows(resid_ref, ctx, last, tok_rows) + delta_ref[...]
+    out_ref[...] = my_half(layer_out, wt).astype(BF)
+    resid = resid_ref[...]
+    scale = norm_scale(resid)
+    normed = resid * scale
+    back = back_ref[...]
+    gain_grad = jnp.sum(back * normed, axis=0, keepdims=True)
+    scaled = back * gains[1:2]
+    mean = jnp.mean(scaled * normed, axis=1, keepdims=True)
+    mid = cot_ref[...].astype(F32) + scale * (scaled - normed * mean)
+    mid_ref[...] = mid
+    mid_bf = mid.astype(BF)
+    mid_bf_ref[...] = mid_bf
+    height = o_ref.shape[0]
+    grad_out_ref[:height] = mul(o_ref[...], my_half(mid_bf, wt)).astype(BF)
+    gain_rows = jnp.broadcast_to(my_half(gain_grad, wt), (16, part_width))
+    grad_out_ref[height:] = gain_rows.astype(BF)
+
+
+def backward_kernel(
+    weights_ref,
+    mid_bf_ref,
+    q_ref,
+    k_ref,
+    v_ref,
+    o_ref,
+    lse_ref,
+    cos_ref,
+    sin_ref,
+    h1_ref,
+    own_ref,
+    got_ref,
+    own_down_ref,
+    got_down_ref,
+    proj_ref,
+    grad_ref,
+    gate_out,
+    up_out,
+    down_out,
+    g_ref,
+    dk_ref,
+    dv_ref,
+    sum_ref,
+    sum_down_ref,
+    sems,
+):
+    rows = q_ref.shape[1]
+    query_width = QUERY_HEADS * HEAD_SIZE
+    pair_width = KEY_VALUE_HEADS * HEAD_SIZE
+    half_dim = HEAD_SIZE // 2
+    for i in range(2):
+        sum_ref[i] = own_ref[i].astype(F32) + got_ref[i].astype(F32)
+    sum_down_ref[...] = own_down_ref[...].astype(F32) + got_down_ref[...].astype(F32)
+    copies = [
+        pltpu.make_async_copy(sum_ref.at[0], gate_out, sems.at[0]),
+        pltpu.make_async_copy(sum_ref.at[1], up_out, sems.at[1]),
+        pltpu.make_async_copy(sum_down_ref, down_out, sems.at[2]),
+    ]
+    for copy in copies:
+        copy.start()
+    g_ref[...] = mul(weights_ref[query_width + 2 * pair_width :], mid_bf_ref[...], NT).astype(BF)
+    repeat = QUERY_HEADS // KEY_VALUE_HEADS
+    tile = min(BACKWARD_TILE, rows)
+    causal = lax.broadcasted_iota(jnp.int32, (tile, tile), 0) <= lax.broadcasted_iota(
+        jnp.int32, (tile, tile), 1
+    )
+
+    def unturn(value, start, stop):
+        cosines, sines = cos_ref[:, start:stop], sin_ref[:, start:stop]
+        low, high = rotated(value[:half_dim], value[half_dim:], cosines, sines, -1.0)
+        return jnp.concatenate([low, high], axis=0).astype(BF)
+
+    def group(g, carry):
+        pair_at = pl.ds(pl.multiple_of(g * HEAD_SIZE, HEAD_SIZE), HEAD_SIZE)
+        keys_t = k_ref[pair_at, :]
+        keys, values = turned(keys_t), turned(v_ref[pair_at, :])
+        dk_ref[...] = jnp.zeros_like(dk_ref)
+        dv_ref[...] = jnp.zeros_like(dv_ref)
+        for r in range(repeat):
+            head = g * repeat + r
+            head_at = pl.ds(pl.multiple_of(head * HEAD_SIZE, HEAD_SIZE), HEAD_SIZE)
+            product = g_ref[head_at, :].astype(F32) * o_ref[head_at, :].astype(F32)
+            delta = jnp.sum(product, axis=0, keepdims=True)
+            for start in range(0, rows, tile):
+                stop = start + tile
+                query, grad = q_ref[head_at, start:stop], g_ref[head_at, start:stop]
+                lse = lse_ref[head, :, start:stop]
+                scores = mul(keys[:stop], query)
+                prob_grad = mul(values[:stop], grad)
+                probs = jnp.where(causal, jnp.exp(scores[start:] - lse), 0.0)
+                if start:
+                    probs = jnp.concatenate([jnp.exp(scores[:start] - lse), probs], axis=0)
+                score_grad = (probs * (prob_grad - delta[:, start:stop])).astype(BF)
+                probs = probs.astype(BF)
+                dq = mul(keys_t[:, :stop], score_grad) * 0.125
+                proj_ref[head_at, start:stop] = unturn(dq, start, stop)
+                dk_ref[:, :stop] += mul(query, score_grad, NT)
+                dv_ref[:, :stop] += mul(grad, probs, NT)
+        key_at = pl.multiple_of(query_width + g * HEAD_SIZE, HEAD_SIZE)
+        proj_ref[pl.ds(key_at, HEAD_SIZE), :] = unturn(dk_ref[...], 0, rows)
+        value_at = pl.multiple_of(query_width + pair_width + g * HEAD_SIZE, HEAD_SIZE)
+        proj_ref[pl.ds(value_at, HEAD_SIZE), :] = dv_ref[...].astype(BF)
+        return carry
+
+    lax.fori_loop(0, KEY_VALUE_HEADS, group, 0)
+    grad_ref[...] = mul(h1_ref[...], proj_ref[...], NT).astype(BF)
+    for copy in copies:
+        copy.wait()
+
+
+def input_kernel(
+    where_ref, proj_ref, weights_ref, x_ref, mid_ref, gain_ref, other_gain_ref, out_ref
+):
+    ctx, wt = where_ref[0], where_ref[1]
+    rows = proj_ref.shape[1]
+    tok_rows, part_width = out_ref.shape
+    last = 2 * rows // tok_rows - 1
+    piece = tok_rows // 4
+    at = lax.broadcasted_iota(jnp.int32, (rows, tok_rows), 0)
+    u = lax.broadcasted_iota(jnp.int32, (rows, tok_rows), 1)
+    j = u // piece
+    base = jnp.where(j % 2 == 0, ctx, last - ctx)
+    position = base * (2 * piece) + (j // 2) * piece + u % piece
+    chosen = jnp.where(at == position, 1.0, 0.0).astype(BF)
+    mine = mul(proj_ref[...], chosen).astype(BF)
+    grad = mul(mine, weights_ref[: proj_ref.shape[0]], TN)
+    gains = in_order(gain_ref[...], other_gain_ref[...], wt, 1)
+    x = own_rows(x_ref, ctx, last, tok_rows).astype(F32)
+    mid = own_rows(mid_ref, ctx, last, tok_rows)
+    scale = norm_scale(x)
+    normed = x * scale
+    scaled = grad * gains[0:1]
+    mean = jnp.mean(scaled * normed, axis=1, keepdims=True)
+    out_ref[...] = my_half(mid + scale * (scaled - normed * mean), wt)
+
+
+def whole_device(layer_input, cotangent, w_qkv, w_out, w_gate, w_up, w_down, gain_attn, gain_mlp):
+    ctx_count = lax.axis_size("ctx")
+    ctx_index = lax.axis_index("ctx")
+    wt_index = lax.axis_index("wt")
+    seq_index = lax.axis_index("seq")
+    where = jnp.stack([ctx_index, wt_index, seq_index]).astype(jnp.int32)
+    tok_rows, part_width = layer_input.shape[1:]
+    full_width = 2 * part_width
+    rows = tok_rows * ctx_count
+    query_width = QUERY_HEADS * HEAD_SIZE
+    pair_width = KEY_VALUE_HEADS * HEAD_SIZE
+    proj_width = query_width + 2 * pair_width
+    hidden = w_gate.shape[1]
+    shape = jax.ShapeDtypeStruct
+
+    def across_ctx(value, distance):
+        return swap(value, "ctx", distance, ctx_count)
+
+    def half_of(value, axis):
+        half = value.shape[axis] // 2
+        return lax.dynamic_slice_in_dim(value, seq_index * half, half, axis)
+
+    block = layer_input[0]
+    row_blocks = block[None]
+    for distance in (4, 2):
+        row_blocks = jnp.concatenate([row_blocks, across_ctx(row_blocks, distance)], axis=0)
+    near = across_ctx(row_blocks, 1)
+    across = swap(row_blocks, "wt", 1, 2)
+    low = swap(near[:2], "wt", 1, 2)
+    high = across_ctx(across[2:], 1)
+
+    projections = jnp.concatenate([w_qkv.T, w_out], axis=0)
+    first = swap(half_of(projections, 0), "wt", 1, 2)
+    second = swap(first, "seq", 1, 2)
+    gains = jnp.stack([gain_attn, gain_mlp])
+    other_gains = swap(gains, "wt", 1, 2)
+
+    cot = cotangent[0][None]
+    cot = jnp.concatenate([cot, swap(cot, "wt", 1, 2)], axis=0)[None]
+    for distance in (1, 2):
+        cot = jnp.concatenate([cot, across_ctx(cot, distance)], axis=0)
+    cot_far = across_ctx(cot, 4)
+
+    mlp = jnp.stack([w_gate.T, w_up.T, w_down])
+    mlp_half, low, high = lax.optimization_barrier((half_of(mlp, 1), low, high))
+    mlp_first = swap(mlp_half, "wt", 1, 2)
+    mlp_second = swap(mlp_first, "seq", 1, 2)
+
+    half_dim = HEAD_SIZE // 2
+    frequency = jnp.power(F32(ROPE_BASE), -jnp.arange(half_dim, dtype=F32) * 2.0 / HEAD_SIZE)
+    angles = frequency[:, None] * jnp.arange(rows, dtype=F32)[None, :]
+    cosines, sines = jnp.cos(angles), jnp.sin(angles)
+
+    x, h1_t, q_t, k_t, v_t, o_t, lse, resid, h2, h2_t, weights = pl.pallas_call(
+        forward_kernel,
+        in_specs=[SMEM] + [VMEM] * 12,
+        out_specs=[VMEM] * 11,
+        out_shape=[
+            shape((rows, full_width), BF),
+            shape((part_width, rows), BF),
+            shape((query_width, rows), BF),
+            shape((pair_width, rows), BF),
+            shape((pair_width, rows), BF),
+            shape((query_width, rows), BF),
+            shape((QUERY_HEADS, 1, rows), F32),
+            shape((rows, full_width), F32),
+            shape((rows, full_width), BF),
+            shape((full_width, rows), BF),
+            shape((proj_width + query_width, full_width), BF),
+        ],
+        scratch_shapes=[
+            pltpu.VMEM((full_width, rows), BF),
+            pltpu.VMEM((proj_width + query_width, part_width), BF),
+        ],
+        name="forward",
+    )(
+        where, row_blocks, near, across, low, high,
+        projections, first, second, gains, other_gains, cosines, sines,
+    )
+
+    cots, grads, grad_down, back, delta = pl.pallas_call(
+        own_mlp_kernel,
+        in_specs=[SMEM] + [VMEM] * 5,
+        out_specs=[VMEM] * 5,
+        out_shape=[
+            shape((rows, full_width), BF),
+            shape((2, full_width, hidden), BF),
+            shape((hidden, full_width), BF),
+            shape((rows, full_width), F32),
+            shape((tok_rows, full_width), F32),
+        ],
+        scratch_shapes=[pltpu.VMEM((rows, HIDDEN_TILE), BF)],
+        name="own_mlp",
+    )(where, cot, cot_far, h2, h2_t, mlp)
+    got = swap(grads, "seq", 1, 2)
+    got_down = swap(grad_down, "seq", 1, 2)
+
+    layer_out, mid, mid_bf, grad_out = pl.pallas_call(
+        other_mlp_kernel,
+        in_specs=[SMEM] + [VMEM] * 10,
+        out_specs=[VMEM] * 4,
+        out_shape=[
+            shape((tok_rows, part_width), BF),
+            shape((rows, full_width), F32),
+            shape((rows, full_width), BF),
+            shape((query_width + 16, part_width), BF),
+        ],
+        scratch_shapes=[
+            pltpu.VMEM((3, hidden, full_width), BF),
+            pltpu.VMEM((rows, HIDDEN_TILE), BF),
+            pltpu.VMEM((rows, full_width), F32),
+            pltpu.VMEM((tok_rows, full_width), F32),
+        ],
+        name="other_mlp",
+    )(where, h2, cots, mlp_first, mlp_second, back, delta, resid, gains, other_gains, o_t)
+    got_out = swap(grad_out, "seq", 1, 2)
+
+    proj_t, grad_qkv, grad_gate, grad_up, grad_down = pl.pallas_call(
+        backward_kernel,
+        in_specs=[VMEM] * 14,
+        out_specs=[VMEM] * 2 + [ANY] * 3,
+        out_shape=[
+            shape((proj_width, rows), BF),
+            shape((part_width, proj_width), BF),
+            shape((full_width, hidden), F32),
+            shape((full_width, hidden), F32),
+            shape((hidden, full_width), F32),
+        ],
+        scratch_shapes=[
+            pltpu.VMEM((query_width, rows), BF),
+            pltpu.VMEM((HEAD_SIZE, rows), F32),
+            pltpu.VMEM((HEAD_SIZE, rows), F32),
+            pltpu.VMEM((2, full_width, hidden), F32),
+            pltpu.VMEM((hidden, full_width), F32),
+            pltpu.SemaphoreType.DMA((3,)),
+        ],
+        name="backward",
+    )(
+        weights, mid_bf, q_t, k_t, v_t, o_t, lse, cosines, sines, h1_t,
+        grads, got, grad_down, got_down,
+    )
+    got_qkv = swap(grad_qkv, "seq", 1, 2)
+    input_grad = pl.pallas_call(
+        input_kernel,
+        in_specs=[SMEM] + [VMEM] * 6,
+        out_specs=VMEM,
+        out_shape=shape((tok_rows, part_width), F32),
+        name="input_grad",
+    )(where, proj_t, weights, x, mid, gains, other_gains)
+
+    out_sum = grad_out.astype(F32) + got_out.astype(F32)
+    qkv_sum = grad_qkv.astype(F32) + got_qkv.astype(F32)
+    grad_gain_attn = jnp.sum(qkv_sum * w_qkv.astype(F32), axis=1) / gain_attn
+    return (
+        layer_out[None],
+        input_grad[None],
+        qkv_sum,
+        out_sum[:query_width],
+        grad_gate,
+        grad_up,
+        grad_down,
+        grad_gain_attn,
+        out_sum[query_width],
+    )
+
+
 def solution(mesh):
     in_specs = (
         P("seq", "ctx", "wt"),
@@ -363,6 +942,8 @@
         P("wt"),
         P("wt"),
     )
+    sizes = mesh.shape
+    whole = sizes["wt"] == 2 and sizes["seq"] == 2 and sizes["ctx"] == 8
     return jax.shard_map(
-        on_device, mesh=mesh, in_specs=in_specs, out_specs=out_specs, check_vma=False
-    )
+        whole_device if whole else split_device, mesh=mesh, in_specs=in_specs, out_specs=out_specs, check_vma=False
+    )

time: 499 us -> 196 us (0.39)
  waiting for transfers between devices: 259 us -> 23 us
  blocking collectives: 120 us -> 0 us
  Pallas kernels: 0 us -> 89.5 us
  matrix products: 39.3 us -> 0 us
  starting transfers between devices: 0.43 us -> 21.7 us
  between operations: 14.8 us -> 0.87 us
    reduce_scatter x5 -> x0, waiting for transfers between devices: 146 us -> none  [the longest x1 117 us: on_device(): lax.psum_scatter(kv_acc, ('ctx', 'wt'), scatter_dimension=1, tiled=True)]
    psum x1 -> x0, waiting for transfers between devices: 113 us -> none  [on_device(): lax.psum((grad_qkv, grad_out, grad_gate, grad_up, grad_down, grad_gain_at...]
    pallas_call x0 -> x5, Pallas kernels: none -> 89.5 us  [the longest x1 26.7 us: whole_device(): pl.pallas_call(backward_kernel, in_specs=[VMEM] * 14, out_specs=[VMEM] *...]
    all_gather x5 -> x0, blocking collectives: 65.8 us -> none  [the longest x1 44.6 us: on_device(): kv_all = lax.all_gather(kv_pair, ('ctx', 'wt'), axis=1, tiled=True)]
    psum x5 -> x0, blocking collectives: 53.9 us -> none  [the longest x1 33.2 us: on_device(): lax.psum((grad_qkv, grad_out, grad_gate, grad_up, grad_down, grad_gain_at...]
    dot_general x36 -> x0, matrix products: 39.3 us -> none  [the longest x6 7.02 us: group_scores(): jnp.einsum('pgrd,kgd->pgrk', query_sel, key_portion, preferred_element_ty...]
    ppermute x0 -> x19, waiting for transfers between devices: none -> 23 us  [swap(): return lax.ppermute(value, axis, [(i, i ^ distance) for i in range(count)])]
    ppermute x0 -> x19, starting transfers between devices: none -> 21.7 us  [swap(): return lax.ppermute(value, axis, [(i, i ^ distance) for i in range(count)])]
  transfers between devices with their start and end apart: 6 -> 19, of which waited for: 6 -> 8; matrix products, arithmetic and copies ran while one was open for 3% -> 27% of each run, Pallas kernels for 0% -> 46%
where the time goes in v1:
time: 196 us; the launch traced here: 195 us
  Pallas kernels  89.5 us (46%)
  local copies, waits for them, and re-layouts  43.7 us (22%)
  waiting for transfers between devices  23 us (12%)
  starting transfers between devices  21.7 us (11%)
  other arithmetic  16 us (8%)
    pallas_call x1, Pallas kernels, whole_device(): pl.pallas_call(backward_kernel, in_specs=[VMEM] * 14, out_specs=[VMEM] *...  26.7 us
    ppermute x19, waiting for transfers between devices, swap(): return lax.ppermute(value, axis, [(i, i ^ distance) for i in range(count)])  23 us
    pallas_call x1, Pallas kernels, whole_device(): pl.pallas_call(forward_kernel, in_specs=[SMEM] + [VMEM] * 12, out_specs=[...  21.9 us
    ppermute x19, starting transfers between devices, swap(): return lax.ppermute(value, axis, [(i, i ^ distance) for i in range(count)])  21.7 us
    pallas_call x1, Pallas kernels, whole_device(): pl.pallas_call(other_mlp_kernel, in_specs=[SMEM] + [VMEM] * 10, out_specs...  18.1 us
    unnamed x55, local copies, waits for them, and re-layouts  17.9 us
    pallas_call x1, Pallas kernels, whole_device(): pl.pallas_call(own_mlp_kernel, in_specs=[SMEM] + [VMEM] * 5, out_specs=[V...  17.3 us
    ppermute x6, local copies, waits for them, and re-layouts, swap(): return lax.ppermute(value, axis, [(i, i ^ distance) for i in range(count)])  14.2 us
  transfers between devices with their start and end apart: 19, of which 8 were waited for; matrix products, arithmetic and copies ran while one was open for 27% of the time, Pallas kernels for 46%

profile of v1, /device:TPU:0, one launch (start us, length us, event | category | flops | bytes accessed | tf_op | source)
XLA Modules:
  0.0 194.7 jit_solution(15899508227838302759)
XLA Ops:
  0.7 1.0 copy.34
  1.7 4.1 %collective-permute-start = (bf16[1,128,288]{2,1,0:T(8,128)(2,1)S(1)}, bf16[1,128,288]{2,1,0:T(8,128)(2,1)S(1)}, u32[]{:S(2)}, u32[]{:S(2)}) collective-permute-start(bf16[1,128,288]{2,1,0:T(8,128)(2,1)S(1)} %copy.34), channel_id=1, source_target_pairs={{0,8},{2,10},{4,12},{6,14},{8,0},{10,2},{12,4},{14,6},{1,9},{3,11}... | collective-permute-start | bytes 221192 | tf_op jit(solution)/shard_map/ppermute | solution.py:360
  5.8 4.9 %collective-permute-done = bf16[1,128,288]{2,1,0:T(8,128)(2,1)S(1)} collective-permute-done((bf16[1,128,288]{2,1,0:T(8,128)(2,1)S(1)}, bf16[1,128,288]{2,1,0:T(8,128)(2,1)S(1)}, u32[]{:S(2)}, u32[]{:S(2)}) %collective-permute-start) | collective-permute-done | bytes 73760 | tf_op jit(solution)/shard_map/ppermute | solution.py:360
  12.8 1.4 copy.38
  16.6 1.5 collective-permute-start.6
  18.1 1.6 copy.44
  20.2 1.3 copy.35
  21.6 1.3 copy.36
  22.9 1.3 copy.37
  24.2 1.8 pad_maximum_fusion.3.rows_ref
  26.0 1.5 collective-permute-start.2
  27.5 1.5 collective-permute-start.3
  29.0 2.3 %pad_maximum_fusion.w_ref = bf16[3,768,576]{2,1,0:T(8,128)(2,1)S(1)} fusion(bf16[1,768,576]{2,1,0:T(8,128)(2,1)} %bitcast.19, bf16[1,768,576]{2,1,0:T(8,128)(2,1)} %bitcast.18, bf16[1,768,576]{2,1,0:T(8,128)(2,1)} %bitcast.17), kind=kLoop, calls=%fused_computation | loop fusion | flops 2654208 | bytes 5308416 | tf_op jit(solution)/shard_map/stack | solution.py:799
  32.1 1.9 maximum_bitcast_fusion
  33.9 1.3 collective-permute-start.10
  35.2 3.0 %collective-permute-done.2.near_ref = bf16[4,128,288]{2,1,0:T(8,128)(2,1)} collective-permute-done((bf16[4,128,288]{2,1,0:T(8,128)(2,1)}, bf16[4,128,288]{2,1,0:T(8,128)(2,1)}, u32[]{:S(2)}, u32[]{:S(2)}) %collective-permute-start.2) | collective-permute-done | bytes 294944 | tf_op jit(solution)/shard_map/ppermute | solution.py:360
  39.2 1.6 collective-permute-start.4
  41.8 1.6 collective-permute-start.5
  43.3 1.2 constant_dynamic-slice_fusion
  45.6 2.0 %collective-permute-done.5.high_ref = bf16[2,128,288]{2,1,0:T(8,128)(2,1)} collective-permute-done((bf16[2,128,288]{2,1,0:T(8,128)(2,1)S(1)}, bf16[2,128,288]{2,1,0:T(8,128)(2,1)}, u32[]{:S(2)}, u32[]{:S(2)}) %collective-permute-start.5) | collective-permute-done | bytes 147488 | tf_op jit(solution)/shard_map/ppermute | solution.py:360
  47.6 3.5 %copy.47 = bf16[3,384,576]{1,2,0:T(8,128)(2,1)} copy(bf16[3,384,576]{2,1,0:T(8,128)(2,1)} %constant_dynamic-slice_fusion) | data formatting | bytes 2654208 | tf_op jit(solution)/shard_map/optimization_barrier | solution.py:800
  51.8 1.1 pad_maximum_fusion.4
  52.9 1.2 collective-permute-start.11
  55.1 5.8 %collective-permute-done.11 = bf16[2,2,128,288]{3,2,1,0:T(8,128)(2,1)S(1)} collective-permute-done((bf16[2,2,128,288]{3,2,1,0:T(8,128)(2,1)S(1)}, bf16[2,2,128,288]{3,2,1,0:T(8,128)(2,1)S(1)}, u32[]{:S(2)}, u32[]{:S(2)}) %collective-permute-start.11) | collective-permute-done | bytes 294944 | tf_op jit(solution)/shard_map/ppermute | solution.py:360
  60.9 1.2 pad_maximum_fusion.2.pairs_ref
  62.1 1.1 copy.45
  63.2 3.4 %collective-permute-start.12 = (bf16[4,2,128,288]{2,3,1,0:T(8,128)(2,1)}, bf16[4,2,128,288]{2,3,1,0:T(8,128)(2,1)}, u32[]{:S(2)}, u32[]{:S(2)}) collective-permute-start(bf16[4,2,128,288]{2,3,1,0:T(8,128)(2,1)} %copy.45), channel_id=1, source_target_pairs={{0,8},{2,10},{4,12},{6,14},{8,0},{10,2},{12,4},{14,6},{1,9},{3,11}... | collective-permute-start | bytes 1769480 | tf_op jit(solution)/shard_map/ppermute | solution.py:360
  66.6 1.3 fusion.1
  67.9 1.1 pad_maximum_fusion.1.proj_ref
  69.6 2.1 %copy.41.first_ref = bf16[768,288]{1,0:T(8,128)(2,1)} copy(bf16[768,288]{0,1:T(8,128)(2,1)} %collective-permute-done.6) | data formatting | bytes 884736 | tf_op jit(solution)/shard_map/ppermute | solution.py:360
  71.7 2.1 %copy.42.second_ref = bf16[768,288]{1,0:T(8,128)(2,1)} copy(bf16[768,288]{0,1:T(8,128)(2,1)} %collective-permute-done.7) | data formatting | bytes 884736 | tf_op jit(solution)/shard_map/ppermute | solution.py:360
  73.7 5.0 %collective-permute-done.8.other_gain_ref = f32[2,288]{1,0:T(2,128)S(1)} collective-permute-done((f32[2,288]{1,0:T(2,128)S(1)}, f32[2,288]{1,0:T(2,128)S(1)}, u32[]{:S(2)}, u32[]{:S(2)}) %collective-permute-start.8) | collective-permute-done | bytes 2336 | tf_op jit(solution)/shard_map/ppermute | solution.py:360
  79.4 21.9 %forward.1 = (bf16[1024,576]{1,0:T(8,128)(2,1)}, bf16[288,1024]{1,0:T(8,128)(2,1)}, bf16[576,1024]{1,0:T(8,128)(2,1)}, bf16[192,1024]{1,0:T(8,128)(2,1)}, bf16[1...) custom-call(s32[3]{0:T(128)} %pad_add_fusion.where_ref, ...), custom_call_target="tpu_custom_call" | custom-call | tf_op jit(solution)/shard_map/forward/pallas_call | solution.py:809
  101.3 2.2 %copy.46.far_ref = bf16[4,2,128,288]{3,2,1,0:T(8,128)(2,1)} copy(bf16[4,2,128,288]{2,3,1,0:T(8,128)(2,1)} %collective-permute-done.12) | data formatting | bytes 1179648 | tf_op jit(solution)/shard_map/ppermute | solution.py:360
  103.5 17.3 %own_mlp.1 = (bf16[1024,576]{1,0:T(8,128)(2,1)}, bf16[2,576,768]{2,1,0:T(8,128)(2,1)}, bf16[768,576]{1,0:T(8,128)(2,1)}, f32[1024,576]{1,0:T(8,128)}, f32[128,576]{1,0:T(8,128)}) custom-call(s32[3]{0:T(128)} %pad_add_fusion.where_ref, bf16[4,2,128,288]{3,2,1,0:T(8,128)(2,1)} %copy-done.1, bf16[4,2,128,288]{3,2,1,0:T(8,128)(2,1)} %copy.46.far_ref, ...), custom_call_target="tpu_custom_call" | custom-call | tf_op jit(solution)/shard_map/own_mlp/pallas_call | solution.py:836
  121.4 2.2 %copy.50 = bf16[768,576]{0,1:T(8,128)(2,1)} copy(bf16[768,576]{1,0:T(8,128)(2,1)} %get-tuple-element.56.own_down_ref) | data formatting | bytes 1769472 | tf_op jit(solution)/shard_map/own_mlp/pallas_call | solution.py:836
  123.7 2.1 %copy.48.first_ref = bf16[3,384,576]{2,1,0:T(8,128)(2,1)} copy(bf16[3,384,576]{1,2,0:T(8,128)(2,1)S(1)} %collective-permute-done.13) | data formatting | bytes 2654208 | tf_op jit(solution)/shard_map/ppermute | solution.py:360
  125.7 1.0 collective-permute-done.14
  126.8 3.5 %copy.49.second_ref = bf16[3,384,576]{2,1,0:T(8,128)(2,1)} copy(bf16[3,384,576]{1,2,0:T(8,128)(2,1)} %collective-permute-done.14) | data formatting | bytes 2654208 | tf_op jit(solution)/shard_map/ppermute | solution.py:360
  130.3 18.1 %other_mlp.1 = (bf16[128,288]{1,0:T(8,128)(2,1)}, f32[1024,576]{1,0:T(8,128)}, bf16[1024,576]{1,0:T(8,128)(2,1)}, bf16[592,288]{1,0:T(8,128)(2,1)}) custom-call(s32[3]{0:T(128)} %pad_add_fusion.where_ref, bf16[1024,576]{1,0:T(8,128)(2,1)} %get-tuple-element.39.h2_ref, bf16[1024,576]{1,0:T(8,128)(2,1)} %get-tuple-element.41.cot_ref, ...), custom_call_target="tpu_custom_call" | custom-call | tf_op jit(solution)/shard_map/other_mlp/pallas_call | solution.py:853
  148.5 2.2 %copy.51.got_down_ref = bf16[768,576]{1,0:T(8,128)(2,1)} copy(bf16[768,576]{0,1:T(8,128)(2,1)} %collective-permute-done.16) | data formatting | bytes 1769472 | tf_op jit(solution)/shard_map/ppermute | solution.py:360
  150.7 1.2 copy-done.5
  152.0 26.7 %backward.1 = (bf16[960,1024]{1,0:T(8,128)(2,1)}, bf16[288,960]{1,0:T(8,128)(2,1)}, f32[576,768]{1,0:T(8,128)}, f32[576,768]{1,0:T(8,128)}, f32[768,576]{1,0:T(8,128)}) custom-call(bf16[1536,576]{1,0:T(8,128)(2,1)} %get-tuple-element.48.weights_ref, bf16[1024,576]{1,0:T(8,128)(2,1)} %get-tuple-element.49.mid_bf_ref, ...), custom_call_target="tpu_custom_call" | custom-call | tf_op jit(solution)/shard_map/backward/pallas_call | solution.py:873
  179.1 2.8 %copy.55 = f32[768,576]{0,1:T(8,128)} copy(f32[768,576]{1,0:T(8,128)} %get-tuple-element.80) | data formatting | bytes 3538944
  181.8 5.5 %input_grad.1 = f32[128,288]{1,0:T(8,128)} custom-call(s32[3]{0:T(128)} %pad_add_fusion.where_ref, bf16[960,1024]{1,0:T(8,128)(2,1)} %get-tuple-element.57.proj_ref, bf16[1536,576]{1,0:T(8,128)(2,1)} %get-tuple-element.48.weights_ref, bf16[1024,576]{1,0:T(8,128)(2,1)} %get-tuple-element.58.x_ref, f32[1024,576]{1,0:T(8,128)} %get-tuple-element.59.mid_ref, ...), custom_call_target="tpu_custom_call" | custom-call | tf_op jit(solution)/shard_map/input_grad/pallas_call | solution.py:898
  187.4 1.7 copy.53
  190.0 1.2 copy.54
  191.8 2.3 %multiply_reduce_fusion = (f32[288]{0:T(512)S(1)}, f32[288,960]{1,0:T(8,128)}) fusion(bf16[288,960]{1,0:T(8,128)(2,1)S(1)} %copy-done.4, bf16[288,960]{1,0:T(8,128)(2,1)} %collective-permute-done.17, bf16[288,960]{1,0:T(8,128)(2,1)S(1)} %copy-done.11), kind=kLoop, calls=%fused_computation.4 | loop fusion | flops 1658592 | bytes 2765952 | tf_op jit(solution)/shard_map/reduce_sum | solution.py:908
  (82 shorter events, 14.7 us)
Async XLA Ops:
  0.6 13.6 %copy-start.15 = (bf16[576,288]{0,1:T(8,128)(2,1)S(1)}, bf16[576,288]{0,1:T(8,128)(2,1)}, u32[]{:S(2)}) copy-start(bf16[576,288]{0,1:T(8,128)(2,1)} %param.12) | copy-start | bytes 995332
  1.7 11.1 %copy-start.9 = (bf16[1,128,288]{2,1,0:T(8,128)(2,1)}, bf16[1,128,288]{2,1,0:T(8,128)(2,1)S(1)}, u32[]{:S(2)}) copy-start(bf16[1,128,288]{2,1,0:T(8,128)(2,1)S(1)} %copy.34) | copy-start | bytes 221188
  1.7 9.0 %collective-permute-start = (bf16[1,128,288]{2,1,0:T(8,128)(2,1)S(1)}, bf16[1,128,288]{2,1,0:T(8,128)(2,1)S(1)}, u32[]{:S(2)}, u32[]{:S(2)}) collective-permute-start(bf16[1,128,288]{2,1,0:T(8,128)(2,1)S(1)} %copy.34), channel_id=1, source_target_pairs={{0,8},{2,10},{4,12},{6,14},{8,0},{10,2},{12,4},{14,6},{1,9},{3,11}... | collective-permute-start | bytes 221192 | tf_op jit(solution)/shard_map/ppermute | solution.py:360
  10.7 0.6 copy-start.13
  12.1 12.1 %collective-permute-start.1 = (bf16[2,128,288]{2,1,0:T(8,128)(2,1)}, bf16[2,128,288]{2,1,0:T(8,128)(2,1)}, u32[]{:S(2)}, u32[]{:S(2)}) collective-permute-start(bf16[2,128,288]{2,1,0:T(8,128)(2,1)} %pad_maximum_fusion.5), channel_id=1, source_target_pairs={{0,4},{2,6},{4,0},{6,2},{8,12},{10,14},{12,8},{14,10},{1,5},{3,7},... | collective-permute-start | bytes 442376 | tf_op jit(solution)/shard_map/ppermute | solution.py:360
  14.3 2.3 %copy-start.2 = (bf16[288,960]{0,1:T(8,128)(2,1)}, bf16[288,960]{0,1:T(8,128)(2,1)S(1)}, u32[]{:S(2)}) copy-start(bf16[288,960]{0,1:T(8,128)(2,1)S(1)} %copy.38) | copy-start | bytes 1658884
  14.5 5.7 %copy-start.6 = (bf16[576,768]{1,0:T(8,128)(2,1)S(1)}, bf16[576,768]{1,0:T(8,128)(2,1)}, u32[]{:S(2)}) copy-start(bf16[576,768]{1,0:T(8,128)(2,1)} %param.13) | copy-start | bytes 2654212
  15.6 6.0 %copy-start.7 = (bf16[576,768]{1,0:T(8,128)(2,1)S(1)}, bf16[576,768]{1,0:T(8,128)(2,1)}, u32[]{:S(2)}) copy-start(bf16[576,768]{1,0:T(8,128)(2,1)} %param.14) | copy-start | bytes 2654212
  16.6 38.5 %collective-permute-start.6 = (bf16[768,288]{0,1:T(8,128)(2,1)}, bf16[768,288]{0,1:T(8,128)(2,1)}, u32[]{:S(2)}, u32[]{:S(2)}) collective-permute-start(bf16[768,288]{0,1:T(8,128)(2,1)} %copy.40), channel_id=1, source_target_pairs={{0,1},{1,0},{2,3},{3,2},{4,5},{5,4},{6,7},{7,6},{8,9},{9,8},{10,11... | collective-permute-start | bytes 1327112 | tf_op jit(solution)/shard_map/ppermute | solution.py:360
  19.7 3.1 %copy-start.8 = (bf16[768,576]{0,1:T(8,128)(2,1)S(1)}, bf16[768,576]{0,1:T(8,128)(2,1)}, u32[]{:S(2)}) copy-start(bf16[768,576]{0,1:T(8,128)(2,1)} %param.15) | copy-start | bytes 2654212
  19.7 12.3 %collective-permute-start.9 = (bf16[1,128,288]{2,1,0:T(8,128)(2,1)}, bf16[1,128,288]{2,1,0:T(8,128)(2,1)}, u32[]{:S(2)}, u32[]{:S(2)}) collective-permute-start(bf16[1,128,288]{2,1,0:T(8,128)(2,1)} %copy.44), channel_id=1, source_target_pairs={{0,1},{1,0},{2,3},{3,2},{4,5},{5,4},{6,7},{7,6},{8,9},{9,8},{10,11... | collective-permute-start | bytes 221192 | tf_op jit(solution)/shard_map/ppermute | solution.py:360
  21.6 2.6 %copy-start.10 = (bf16[1,128,288]{2,1,0:T(8,128)(2,1)S(1)}, bf16[1,128,288]{2,1,0:T(8,128)(2,1)}, u32[]{:S(2)}) copy-start(bf16[1,128,288]{2,1,0:T(8,128)(2,1)} %copy-done.9) | copy-start | bytes 221188
  21.6 2.6 %copy-start.14 = (bf16[1,128,288]{2,1,0:T(8,128)(2,1)S(1)}, bf16[1,128,288]{2,1,0:T(8,128)(2,1)}, u32[]{:S(2)}) copy-start(bf16[1,128,288]{2,1,0:T(8,128)(2,1)} %copy-done.13) | copy-start | bytes 221188
  26.0 12.3 %collective-permute-start.2 = (bf16[4,128,288]{2,1,0:T(8,128)(2,1)}, bf16[4,128,288]{2,1,0:T(8,128)(2,1)}, u32[]{:S(2)}, u32[]{:S(2)}) collective-permute-start(bf16[4,128,288]{2,1,0:T(8,128)(2,1)} %pad_maximum_fusion.3.rows_ref), channel_id=1, source_target_pairs={{0,2},{2,0},{4,6},{6,4},{8,10},{10,8},{12,14},{14,12},{1,3},{3,1},... | collective-permute-start | bytes 884744 | tf_op jit(solution)/shard_map/ppermute | solution.py:360
  27.5 13.3 %collective-permute-start.3 = (bf16[4,128,288]{2,1,0:T(8,128)(2,1)}, bf16[4,128,288]{2,1,0:T(8,128)(2,1)}, u32[]{:S(2)}, u32[]{:S(2)}) collective-permute-start(bf16[4,128,288]{2,1,0:T(8,128)(2,1)} %pad_maximum_fusion.3.rows_ref), channel_id=1, source_target_pairs={{0,1},{1,0},{2,3},{3,2},{4,5},{5,4},{6,7},{7,6},{8,9},{9,8},{10,11... | collective-permute-start | bytes 884744 | tf_op jit(solution)/shard_map/ppermute | solution.py:360
  31.3 13.3 %copy-start = (bf16[3,768,576]{2,1,0:T(8,128)(2,1)}, bf16[3,768,576]{2,1,0:T(8,128)(2,1)S(1)}, u32[]{:S(2)}) copy-start(bf16[3,768,576]{2,1,0:T(8,128)(2,1)S(1)} %pad_maximum_fusion.w_ref) | copy-start | bytes 7962628
  33.9 17.9 %collective-permute-start.10 = (bf16[1,2,128,288]{3,2,1,0:T(8,128)(2,1)}, bf16[1,2,128,288]{3,2,1,0:T(8,128)(2,1)}, u32[]{:S(2)}, u32[]{:S(2)}) collective-permute-start(bf16[1,2,128,288]{3,2,1,0:T(8,128)(2,1)} %maximum_bitcast_fusion), channel_id=1, source_target_pairs={{0,2},{2,0},{4,6},{6,4},{8,10},{10,8},{12,14},{14,12},{1,3},{3,1},... | collective-permute-start | bytes 442376 | tf_op jit(solution)/shard_map/ppermute | solution.py:360
  39.2 5.7 %collective-permute-start.4 = (bf16[2,128,288]{2,1,0:T(8,128)(2,1)S(1)}, bf16[2,128,288]{2,1,0:T(8,128)(2,1)S(1)}, u32[]{:S(2)}, u32[]{:S(2)}) collective-permute-start(bf16[2,128,288]{2,1,0:T(8,128)(2,1)S(1)} %slice.16), channel_id=1, source_target_pairs={{0,1},{1,0},{2,3},{3,2},{4,5},{5,4},{6,7},{7,6},{8,9},{9,8},{10,11... | collective-permute-start | bytes 442376 | tf_op jit(solution)/shard_map/ppermute | solution.py:360
  41.8 5.8 %collective-permute-start.5 = (bf16[2,128,288]{2,1,0:T(8,128)(2,1)S(1)}, bf16[2,128,288]{2,1,0:T(8,128)(2,1)}, u32[]{:S(2)}, u32[]{:S(2)}) collective-permute-start(bf16[2,128,288]{2,1,0:T(8,128)(2,1)S(1)} %slice.17), channel_id=1, source_target_pairs={{0,2},{2,0},{4,6},{6,4},{8,10},{10,8},{12,14},{14,12},{1,3},{3,1},... | collective-permute-start | bytes 442376 | tf_op jit(solution)/shard_map/ppermute | solution.py:360
  44.6 9.6 %copy-start.20 = (f32[288]{0:T(512)S(1)}, f32[288]{0:T(512)}, u32[]{:S(2)}) copy-start(f32[288]{0:T(512)} %param.16) | copy-start | bytes 3460
  44.6 9.6 %copy-start.21 = (f32[288]{0:T(512)S(1)}, f32[288]{0:T(512)}, u32[]{:S(2)}) copy-start(f32[288]{0:T(512)} %param.17) | copy-start | bytes 3460
  44.9 0.7 copy-start.16
  51.1 69.7 %collective-permute-start.13 = (bf16[3,384,576]{1,2,0:T(8,128)(2,1)}, bf16[3,384,576]{1,2,0:T(8,128)(2,1)S(1)}, u32[]{:S(2)}, u32[]{:S(2)}) collective-permute-start(bf16[3,384,576]{1,2,0:T(8,128)(2,1)} %copy.47), channel_id=1, source_target_pairs={{0,1},{1,0},{2,3},{3,2},{4,5},{5,4},{6,7},{7,6},{8,9},{9,8},{10,11... | collective-permute-start | bytes 3981320 | tf_op jit(solution)/shard_map/ppermute | solution.py:360
  52.9 8.0 %collective-permute-start.11 = (bf16[2,2,128,288]{3,2,1,0:T(8,128)(2,1)S(1)}, bf16[2,2,128,288]{3,2,1,0:T(8,128)(2,1)S(1)}, u32[]{:S(2)}, u32[]{:S(2)}) collective-permute-start(bf16[2,2,128,288]{3,2,1,0:T(8,128)(2,1)S(1)} %pad_maximum_fusion.4), channel_id=1, source_target_pairs={{0,4},{2,6},{4,0},{6,2},{8,12},{10,14},{12,8},{14,10},{1,5},{3,7},... | collective-permute-start | bytes 884744 | tf_op jit(solution)/shard_map/ppermute | solution.py:360
  54.2 9.1 %copy-start.18 = (f32[2,288]{1,0:T(2,128)}, f32[2,288]{1,0:T(2,128)S(1)}, u32[]{:S(2)}) copy-start(f32[2,288]{1,0:T(2,128)S(1)} %pad_maximum_fusion.6.gain_ref) | copy-start | bytes 6916
  54.2 24.6 %collective-permute-start.8 = (f32[2,288]{1,0:T(2,128)S(1)}, f32[2,288]{1,0:T(2,128)S(1)}, u32[]{:S(2)}, u32[]{:S(2)}) collective-permute-start(f32[2,288]{1,0:T(2,128)S(1)} %pad_maximum_fusion.6.gain_ref), channel_id=1, source_target_pairs={{0,1},{1,0},{2,3},{3,2},{4,5},{5,4},{6,7},{7,6},{8,9},{9,8},{10,11... | collective-permute-start | bytes 6920 | tf_op jit(solution)/shard_map/ppermute | solution.py:360
  55.0 12.8 %copy-start.3 = (bf16[288,960]{0,1:T(8,128)(2,1)S(1)}, bf16[288,960]{0,1:T(8,128)(2,1)}, u32[]{:S(2)}) copy-start(bf16[288,960]{0,1:T(8,128)(2,1)} %copy-done.2) | copy-start | bytes 1658884
  55.1 16.6 %collective-permute-start.7 = (bf16[768,288]{0,1:T(8,128)(2,1)}, bf16[768,288]{0,1:T(8,128)(2,1)}, u32[]{:S(2)}, u32[]{:S(2)}) collective-permute-start(bf16[768,288]{0,1:T(8,128)(2,1)} %collective-permute-done.6), channel_id=1, source_target_pairs={{0,16},{16,0},{1,17},{17,1},{2,18},{18,2},{3,19},{19,3},{4,20},{20... | collective-permute-start | bytes 1327112 | tf_op jit(solution)/shard_map/ppermute | solution.py:360
  62.1 6.9 %copy-start.1 = (bf16[4,2,128,288]{3,2,1,0:T(8,128)(2,1)}, bf16[4,2,128,288]{3,2,1,0:T(8,128)(2,1)S(1)}, u32[]{:S(2)}) copy-start(bf16[4,2,128,288]{3,2,1,0:T(8,128)(2,1)S(1)} %pad_maximum_fusion.2.pairs_ref) | copy-start | bytes 1769476
  63.2 38.1 %collective-permute-start.12 = (bf16[4,2,128,288]{2,3,1,0:T(8,128)(2,1)}, bf16[4,2,128,288]{2,3,1,0:T(8,128)(2,1)}, u32[]{:S(2)}, u32[]{:S(2)}) collective-permute-start(bf16[4,2,128,288]{2,3,1,0:T(8,128)(2,1)} %copy.45), channel_id=1, source_target_pairs={{0,8},{2,10},{4,12},{6,14},{8,0},{10,2},{12,4},{14,6},{1,9},{3,11}... | collective-permute-start | bytes 1769480 | tf_op jit(solution)/shard_map/ppermute | solution.py:360
  78.8 0.6 copy-start.19
  120.8 29.9 %collective-permute-start.15 = (bf16[2,576,768]{2,1,0:T(8,128)(2,1)}, bf16[2,576,768]{2,1,0:T(8,128)(2,1)S(1)}, u32[]{:S(2)}, u32[]{:S(2)}) collective-permute-start(bf16[2,576,768]{2,1,0:T(8,128)(2,1)} %get-tuple-element.55.own_ref), channel_id=1, source_target_pairs={{0,16},{16,0},{1,17},{17,1},{2,18},{18,2},{3,19},{19,3},{4,20},{20... | collective-permute-start | bytes 5308424 | tf_op jit(solution)/shard_map/ppermute | solution.py:360
  120.8 5.9 %collective-permute-start.14 = (bf16[3,384,576]{1,2,0:T(8,128)(2,1)S(1)}, bf16[3,384,576]{1,2,0:T(8,128)(2,1)}, u32[]{:S(2)}, u32[]{:S(2)}) collective-permute-start(bf16[3,384,576]{1,2,0:T(8,128)(2,1)S(1)} %collective-permute-done.13), channel_id=1, source_target_pairs={{0,16},{16,0},{1,17},{17,1},{2,18},{18,2},{3,19},{19,3},{4,20},{20... | collective-permute-start | bytes 3981320 | tf_op jit(solution)/shard_map/ppermute | solution.py:360
  123.6 24.9 %collective-permute-start.16 = (bf16[768,576]{0,1:T(8,128)(2,1)}, bf16[768,576]{0,1:T(8,128)(2,1)}, u32[]{:S(2)}, u32[]{:S(2)}) collective-permute-start(bf16[768,576]{0,1:T(8,128)(2,1)} %copy.50), channel_id=1, source_target_pairs={{0,16},{16,0},{1,17},{17,1},{2,18},{18,2},{3,19},{19,3},{4,20},{20... | collective-permute-start | bytes 2654216 | tf_op jit(solution)/shard_map/ppermute | solution.py:360
  148.4 41.5 %collective-permute-start.18 = (bf16[592,288]{1,0:T(8,128)(2,1)}, bf16[592,288]{1,0:T(8,128)(2,1)S(1)}, u32[]{:S(2)}, u32[]{:S(2)}) collective-permute-start(bf16[592,288]{1,0:T(8,128)(2,1)} %get-tuple-element.61), channel_id=1, source_target_pairs={{0,16},{16,0},{1,17},{17,1},{2,18},{18,2},{3,19},{19,3},{4,20},{20... | collective-permute-start | bytes 1022984 | tf_op jit(solution)/shard_map/ppermute | solution.py:360
  150.7 1.2 copy-start.5
  178.7 13.1 %collective-permute-start.17 = (bf16[288,960]{1,0:T(8,128)(2,1)}, bf16[288,960]{1,0:T(8,128)(2,1)}, u32[]{:S(2)}, u32[]{:S(2)}) collective-permute-start(bf16[288,960]{1,0:T(8,128)(2,1)} %get-tuple-element.60), channel_id=1, source_target_pairs={{0,16},{16,0},{1,17},{17,1},{2,18},{18,2},{3,19},{19,3},{4,20},{20... | collective-permute-start | bytes 1658888 | tf_op jit(solution)/shard_map/ppermute | solution.py:360
  181.8 7.2 %copy-start.17 = (bf16[128,288]{1,0:T(8,128)(2,1)S(1)}, bf16[128,288]{1,0:T(8,128)(2,1)}, u32[]{:S(2)}) copy-start(bf16[128,288]{1,0:T(8,128)(2,1)} %get-tuple-element.47) | copy-start | bytes 221188
  181.8 8.0 %copy-start.12 = (bf16[592,288]{1,0:T(8,128)(2,1)S(1)}, bf16[592,288]{1,0:T(8,128)(2,1)}, u32[]{:S(2)}) copy-start(bf16[592,288]{1,0:T(8,128)(2,1)} %get-tuple-element.61) | copy-start | bytes 1022980
  189.9 1.9 copy-start.4
  189.9 1.9 copy-start.11

commit v2 on v1

--- a/solution.py
+++ b/solution.py
@@ -345,7 +345,7 @@
 FORWARD_TILE = 512
 BACKWARD_TILE = 256
 HIDDEN_TILE = 256
-ROW_DISTANCES = (0, 4, 2, 6)
+MIB = 1 << 20
 NN = (((1,), (0,)), ((), ()))
 NT = (((1,), (1,)), ((), ()))
 TN = (((0,), (0,)), ((), ()))
@@ -409,14 +409,20 @@
 
 def forward_kernel(
     where_ref,
-    rows_ref,
-    near_ref,
-    across_ref,
+    one_ref,
+    two_ref,
+    near_one_ref,
+    near_two_ref,
+    across_one_ref,
+    across_two_ref,
     low_ref,
     high_ref,
     proj_ref,
     first_ref,
     second_ref,
+    out_ref,
+    out_first_ref,
+    out_second_ref,
     gain_ref,
     other_gain_ref,
     cos_ref,
@@ -433,28 +439,38 @@
     h2t_ref,
     weights_ref,
     h1t_ref,
-    other_ref,
+    flat_ref,
+    flat_out_ref,
 ):
     ctx, wt, seq = where_ref[0], where_ref[1], where_ref[2]
-    count, tok_rows, part_width = rows_ref.shape
-    last = 4 * count - 1
+    part_width = one_ref.shape[1]
     rows = x_ref.shape[0]
+    last = 2 * rows // one_ref.shape[2] - 1
     query_width = QUERY_HEADS * HEAD_SIZE
     pair_width = KEY_VALUE_HEADS * HEAD_SIZE
     half_dim = HEAD_SIZE // 2
-    for k in range(count):
-        for d in range(2):
-            own = rows_ref[k] if d == 0 else near_ref[k]
-            if d == 0:
-                other = across_ref[k]
-            else:
-                other = low_ref[k] if k < count // 2 else high_ref[k - count // 2]
-            owner = jnp.bitwise_xor(ctx, ROW_DISTANCES[k] + d)
-            store_rows(x_ref, in_order(own, other, wt, 1), owner, last)
-    half = first_ref.shape[0]
-    other_ref[pl.ds(pl.multiple_of(seq * half, 16), half), :] = first_ref[...]
-    other_ref[pl.ds(pl.multiple_of((1 - seq) * half, 16), half), :] = second_ref[...]
-    weights_ref[...] = in_order(proj_ref[...], other_ref[...], wt, 1)
+    sources = (
+        (one_ref, across_one_ref, 0),
+        (two_ref, across_two_ref, 2),
+        (near_one_ref, low_ref, 1),
+        (near_two_ref, high_ref, 3),
+    )
+    for own, other, distance in sources:
+        for i in range(2):
+            full = turned(in_order(own[i], other[i], wt, 0))
+            store_rows(x_ref, full, jnp.bitwise_xor(ctx, distance + 4 * i), last)
+
+    def assemble(out, own, first, second):
+        half = first.shape[0]
+        out[pl.ds(pl.multiple_of(wt * 2 * half, 16), 2 * half), :] = own[...]
+        base = (1 - wt) * 2 * half
+        out[pl.ds(pl.multiple_of(base + seq * half, 16), half), :] = first[...]
+        out[pl.ds(pl.multiple_of(base + (1 - seq) * half, 16), half), :] = second[...]
+
+    assemble(flat_ref, proj_ref, first_ref, second_ref)
+    assemble(flat_out_ref, out_ref, out_first_ref, out_second_ref)
+    weights_ref[: query_width + 2 * pair_width] = turned(flat_ref[...])
+    weights_ref[query_width + 2 * pair_width :] = turned(flat_out_ref[...])
     gains = in_order(gain_ref[...], other_gain_ref[...], wt, 1)
     x = x_ref[...].astype(F32)
     hidden_one = x * norm_scale(x) * gains[0:1]
@@ -517,15 +533,15 @@
 
 
 def mlp_chunk(hidden_two, cots, gate, up, down):
-    gate_pre = mul(hidden_two, gate, NT)
-    up_pre = mul(hidden_two, up, NT)
-    act_grad = mul(cots, down, NT)
+    gate_pre = mul(hidden_two, gate)
+    up_pre = mul(hidden_two, up)
+    act_grad = mul(cots, down)
     sigmoid_gate = jax.nn.sigmoid(gate_pre)
     silu = gate_pre * sigmoid_gate
     activated = (silu * up_pre).astype(BF)
     gate_grad = (act_grad * up_pre * (sigmoid_gate + silu * (1.0 - sigmoid_gate))).astype(BF)
     up_grad = (act_grad * silu).astype(BF)
-    back = mul(gate_grad, gate) + mul(up_grad, up)
+    back = mul(gate_grad, gate, NT) + mul(up_grad, up, NT)
     return activated, gate_grad, up_grad, back
 
 
@@ -535,38 +551,41 @@
     far_ref,
     h2_ref,
     h2t_ref,
-    w_ref,
+    gate_ref,
+    up_ref,
+    down_ref,
     cot_ref,
     grads_ref,
-    grad_down_ref,
     back_ref,
     delta_ref,
     act_ref,
+    cott_ref,
 ):
     ctx, wt = where_ref[0], where_ref[1]
-    count, _, tok_rows, part_width = pairs_ref.shape
+    count, _, part_width, tok_rows = pairs_ref.shape
     last = 4 * count - 1
     for k in range(2 * count):
         ref = pairs_ref if k < count else far_ref
-        full = in_order(ref[k % count, 0], ref[k % count, 1], wt, 1)
+        full = turned(in_order(ref[k % count, 0], ref[k % count, 1], wt, 0))
         store_rows(cot_ref, full, jnp.bitwise_xor(ctx, k), last)
-    hidden = w_ref.shape[1]
+    cott_ref[...] = turned(cot_ref[...])
+    hidden = gate_ref.shape[1]
     tile = HIDDEN_TILE
     back_ref[...] = jnp.zeros_like(back_ref)
     delta_ref[...] = jnp.zeros_like(delta_ref)
 
     def chunk(j, carry):
         at = pl.ds(pl.multiple_of(j * tile, tile), tile)
-        down = w_ref[2, at, :]
+        down = down_ref[:, at]
         activated, gate_grad, up_grad, back = mlp_chunk(
-            h2_ref[...], cot_ref[...], w_ref[0, at, :], w_ref[1, at, :], down
+            h2_ref[...], cot_ref[...], gate_ref[:, at], up_ref[:, at], down
         )
         back_ref[...] += back
         act_ref[...] = activated
-        delta_ref[...] += mul(own_rows(act_ref, ctx, last, tok_rows), down)
+        delta_ref[...] += mul(own_rows(act_ref, ctx, last, tok_rows), down, NT)
         grads_ref[0, :, at] = mul(h2t_ref[...], gate_grad).astype(BF)
         grads_ref[1, :, at] = mul(h2t_ref[...], up_grad).astype(BF)
-        grad_down_ref[at, :] = mul(activated, cot_ref[...], TN).astype(BF)
+        grads_ref[2, :, at] = mul(cott_ref[...], activated).astype(BF)
         return carry
 
     lax.fori_loop(0, hidden // tile, chunk, 0)
@@ -595,30 +614,31 @@
 ):
     ctx, wt = where_ref[0], where_ref[1]
     rows = h2_ref.shape[0]
-    tok_rows, part_width = out_ref.shape
+    seq = where_ref[2]
+    part_width, tok_rows = out_ref.shape
     last = 2 * rows // tok_rows - 1
     half = first_ref.shape[1]
-    w_ref[:, :half] = first_ref[...]
-    w_ref[:, half:] = second_ref[...]
+    w_ref[:, pl.ds(pl.multiple_of(seq * half, 16), half), :] = first_ref[...]
+    w_ref[:, pl.ds(pl.multiple_of((1 - seq) * half, 16), half), :] = second_ref[...]
     tile = HIDDEN_TILE
     back_ref[...] = back_in_ref[...]
     delta_ref[...] = delta_in_ref[...]
 
     def chunk(j, carry):
         at = pl.ds(pl.multiple_of(j * tile, tile), tile)
-        down = w_ref[2, at, :]
+        down = w_ref[2, :, at]
         activated, _, _, back = mlp_chunk(
-            h2_ref[...], cot_ref[...], w_ref[0, at, :], w_ref[1, at, :], down
+            h2_ref[...], cot_ref[...], w_ref[0, :, at], w_ref[1, :, at], down
         )
         back_ref[...] += back
         act_ref[...] = activated
-        delta_ref[...] += mul(own_rows(act_ref, ctx, last, tok_rows), down)
+        delta_ref[...] += mul(own_rows(act_ref, ctx, last, tok_rows), down, NT)
         return carry
 
-    lax.fori_loop(0, 2 * half // tile, chunk, 0)
+    lax.fori_loop(0, first_ref.shape[2] // tile, chunk, 0)
     gains = in_order(gain_ref[...], other_gain_ref[...], wt, 1)
     layer_out = own_rows(resid_ref, ctx, last, tok_rows) + delta_ref[...]
-    out_ref[...] = my_half(layer_out, wt).astype(BF)
+    out_ref[...] = my_half(layer_out, wt).T.astype(BF)
     resid = resid_ref[...]
     scale = norm_scale(resid)
     normed = resid * scale
@@ -630,10 +650,10 @@
     mid_ref[...] = mid
     mid_bf = mid.astype(BF)
     mid_bf_ref[...] = mid_bf
-    height = o_ref.shape[0]
-    grad_out_ref[:height] = mul(o_ref[...], my_half(mid_bf, wt)).astype(BF)
-    gain_rows = jnp.broadcast_to(my_half(gain_grad, wt), (16, part_width))
-    grad_out_ref[height:] = gain_rows.astype(BF)
+    mid_t = mid.T
+    mine = jnp.where(wt == 0, mid_t[:part_width], mid_t[part_width:]).astype(BF)
+    grad_out_ref[:part_width] = mul(mine, o_ref[...], NT).astype(BF)
+    grad_out_ref[part_width:] = jnp.broadcast_to(gain_grad, (16, gain_grad.shape[1])).astype(BF)
 
 
 def backward_kernel(
@@ -649,8 +669,6 @@
     h1_ref,
     own_ref,
     got_ref,
-    own_down_ref,
-    got_down_ref,
     proj_ref,
     grad_ref,
     gate_out,
@@ -660,21 +678,16 @@
     dk_ref,
     dv_ref,
     sum_ref,
-    sum_down_ref,
     sems,
 ):
     rows = q_ref.shape[1]
     query_width = QUERY_HEADS * HEAD_SIZE
     pair_width = KEY_VALUE_HEADS * HEAD_SIZE
     half_dim = HEAD_SIZE // 2
-    for i in range(2):
+    copies = []
+    for i, out in enumerate((gate_out, up_out, down_out)):
         sum_ref[i] = own_ref[i].astype(F32) + got_ref[i].astype(F32)
-    sum_down_ref[...] = own_down_ref[...].astype(F32) + got_down_ref[...].astype(F32)
-    copies = [
-        pltpu.make_async_copy(sum_ref.at[0], gate_out, sems.at[0]),
-        pltpu.make_async_copy(sum_ref.at[1], up_out, sems.at[1]),
-        pltpu.make_async_copy(sum_down_ref, down_out, sems.at[2]),
-    ]
+        copies.append(pltpu.make_async_copy(sum_ref.at[i], out, sems.at[i]))
     for copy in copies:
         copy.start()
     g_ref[...] = mul(weights_ref[query_width + 2 * pair_width :], mid_bf_ref[...], NT).astype(BF)
@@ -732,7 +745,7 @@
 ):
     ctx, wt = where_ref[0], where_ref[1]
     rows = proj_ref.shape[1]
-    tok_rows, part_width = out_ref.shape
+    part_width, tok_rows = out_ref.shape
     last = 2 * rows // tok_rows - 1
     piece = tok_rows // 4
     at = lax.broadcasted_iota(jnp.int32, (rows, tok_rows), 0)
@@ -750,7 +763,7 @@
     normed = x * scale
     scaled = grad * gains[0:1]
     mean = jnp.mean(scaled * normed, axis=1, keepdims=True)
-    out_ref[...] = my_half(mid + scale * (scaled - normed * mean), wt)
+    out_ref[...] = my_half(mid + scale * (scaled - normed * mean), wt).T
 
 
 def whole_device(layer_input, cotangent, w_qkv, w_out, w_gate, w_up, w_down, gain_attn, gain_mlp):
@@ -775,29 +788,30 @@
         half = value.shape[axis] // 2
         return lax.dynamic_slice_in_dim(value, seq_index * half, half, axis)
 
-    block = layer_input[0]
-    row_blocks = block[None]
-    for distance in (4, 2):
-        row_blocks = jnp.concatenate([row_blocks, across_ctx(row_blocks, distance)], axis=0)
-    near = across_ctx(row_blocks, 1)
-    across = swap(row_blocks, "wt", 1, 2)
-    low = swap(near[:2], "wt", 1, 2)
-    high = across_ctx(across[2:], 1)
-
-    projections = jnp.concatenate([w_qkv.T, w_out], axis=0)
-    first = swap(half_of(projections, 0), "wt", 1, 2)
+    gains = jnp.stack([gain_attn, gain_mlp])
+    block = layer_input[0].T
+    one = jnp.stack([block, across_ctx(block, 4)])
+    two = across_ctx(one, 2)
+    near_one, across_one = across_ctx(one, 1), swap(one, "wt", 1, 2)
+    near_two, across_two = across_ctx(two, 1), swap(two, "wt", 1, 2)
+    low = swap(near_one, "wt", 1, 2)
+    high = across_ctx(across_two, 1)
+
+    other_gains = swap(gains, "wt", 1, 2)
+    first = swap(half_of(w_qkv, 0), "wt", 1, 2)
     second = swap(first, "seq", 1, 2)
-    gains = jnp.stack([gain_attn, gain_mlp])
-    other_gains = swap(gains, "wt", 1, 2)
-
-    cot = cotangent[0][None]
-    cot = jnp.concatenate([cot, swap(cot, "wt", 1, 2)], axis=0)[None]
+    out_first = swap(half_of(w_out.T, 0), "wt", 1, 2)
+    out_second = swap(out_first, "seq", 1, 2)
+
+    cot = cotangent[0].T
+    cot = jnp.stack([cot, swap(cot, "wt", 1, 2)])[None]
     for distance in (1, 2):
         cot = jnp.concatenate([cot, across_ctx(cot, distance)], axis=0)
     cot_far = across_ctx(cot, 4)
 
-    mlp = jnp.stack([w_gate.T, w_up.T, w_down])
-    mlp_half, low, high = lax.optimization_barrier((half_of(mlp, 1), low, high))
+    down_t = w_down.T
+    mlp_half = jnp.stack([half_of(w_gate, 0), half_of(w_up, 0), half_of(down_t, 0)])
+    mlp_half, low, high = lax.optimization_barrier((mlp_half, low, high))
     mlp_first = swap(mlp_half, "wt", 1, 2)
     mlp_second = swap(mlp_first, "seq", 1, 2)
 
@@ -808,7 +822,7 @@
 
     x, h1_t, q_t, k_t, v_t, o_t, lse, resid, h2, h2_t, weights = pl.pallas_call(
         forward_kernel,
-        in_specs=[SMEM] + [VMEM] * 12,
+        in_specs=[SMEM] + [VMEM] * 18,
         out_specs=[VMEM] * 11,
         out_shape=[
             shape((rows, full_width), BF),
@@ -825,43 +839,46 @@
         ],
         scratch_shapes=[
             pltpu.VMEM((full_width, rows), BF),
-            pltpu.VMEM((proj_width + query_width, part_width), BF),
+            pltpu.VMEM((full_width, proj_width), BF),
+            pltpu.VMEM((full_width, query_width), BF),
         ],
         name="forward",
     )(
-        where, row_blocks, near, across, low, high,
-        projections, first, second, gains, other_gains, cosines, sines,
-    )
-
-    cots, grads, grad_down, back, delta = pl.pallas_call(
+        where, one, two, near_one, near_two, across_one, across_two, low, high,
+        w_qkv, first, second, w_out.T, out_first, out_second,
+        gains, other_gains, cosines, sines,
+    )
+
+    cots, grads, back, delta = pl.pallas_call(
         own_mlp_kernel,
-        in_specs=[SMEM] + [VMEM] * 5,
-        out_specs=[VMEM] * 5,
+        in_specs=[SMEM] + [VMEM] * 7,
+        out_specs=[VMEM] * 4,
         out_shape=[
             shape((rows, full_width), BF),
-            shape((2, full_width, hidden), BF),
-            shape((hidden, full_width), BF),
+            shape((3, full_width, hidden), BF),
             shape((rows, full_width), F32),
             shape((tok_rows, full_width), F32),
         ],
-        scratch_shapes=[pltpu.VMEM((rows, HIDDEN_TILE), BF)],
+        scratch_shapes=[
+            pltpu.VMEM((rows, HIDDEN_TILE), BF),
+            pltpu.VMEM((full_width, rows), BF),
+        ],
         name="own_mlp",
-    )(where, cot, cot_far, h2, h2_t, mlp)
+    )(where, cot, cot_far, h2, h2_t, w_gate, w_up, down_t)
     got = swap(grads, "seq", 1, 2)
-    got_down = swap(grad_down, "seq", 1, 2)
 
     layer_out, mid, mid_bf, grad_out = pl.pallas_call(
         other_mlp_kernel,
         in_specs=[SMEM] + [VMEM] * 10,
         out_specs=[VMEM] * 4,
         out_shape=[
-            shape((tok_rows, part_width), BF),
+            shape((part_width, tok_rows), BF),
             shape((rows, full_width), F32),
             shape((rows, full_width), BF),
-            shape((query_width + 16, part_width), BF),
+            shape((part_width + 16, query_width), BF),
         ],
         scratch_shapes=[
-            pltpu.VMEM((3, hidden, full_width), BF),
+            pltpu.VMEM((3, full_width, hidden), BF),
             pltpu.VMEM((rows, HIDDEN_TILE), BF),
             pltpu.VMEM((rows, full_width), F32),
             pltpu.VMEM((tok_rows, full_width), F32),
@@ -870,52 +887,52 @@
     )(where, h2, cots, mlp_first, mlp_second, back, delta, resid, gains, other_gains, o_t)
     got_out = swap(grad_out, "seq", 1, 2)
 
-    proj_t, grad_qkv, grad_gate, grad_up, grad_down = pl.pallas_call(
+    proj_t, grad_qkv, grad_gate, grad_up, grad_down_t = pl.pallas_call(
         backward_kernel,
-        in_specs=[VMEM] * 14,
+        in_specs=[VMEM] * 12,
         out_specs=[VMEM] * 2 + [ANY] * 3,
         out_shape=[
             shape((proj_width, rows), BF),
             shape((part_width, proj_width), BF),
             shape((full_width, hidden), F32),
             shape((full_width, hidden), F32),
-            shape((hidden, full_width), F32),
+            shape((full_width, hidden), F32),
         ],
         scratch_shapes=[
             pltpu.VMEM((query_width, rows), BF),
             pltpu.VMEM((HEAD_SIZE, rows), F32),
             pltpu.VMEM((HEAD_SIZE, rows), F32),
-            pltpu.VMEM((2, full_width, hidden), F32),
-            pltpu.VMEM((hidden, full_width), F32),
+            pltpu.VMEM((3, full_width, hidden), F32),
             pltpu.SemaphoreType.DMA((3,)),
         ],
         name="backward",
     )(
         weights, mid_bf, q_t, k_t, v_t, o_t, lse, cosines, sines, h1_t,
-        grads, got, grad_down, got_down,
+        grads, got,
     )
     got_qkv = swap(grad_qkv, "seq", 1, 2)
     input_grad = pl.pallas_call(
         input_kernel,
         in_specs=[SMEM] + [VMEM] * 6,
         out_specs=VMEM,
-        out_shape=shape((tok_rows, part_width), F32),
+        out_shape=shape((part_width, tok_rows), F32),
         name="input_grad",
     )(where, proj_t, weights, x, mid, gains, other_gains)
 
     out_sum = grad_out.astype(F32) + got_out.astype(F32)
     qkv_sum = grad_qkv.astype(F32) + got_qkv.astype(F32)
     grad_gain_attn = jnp.sum(qkv_sum * w_qkv.astype(F32), axis=1) / gain_attn
+    grad_gain_mlp = lax.dynamic_slice_in_dim(out_sum[part_width], wt_index * part_width, part_width)
     return (
-        layer_out[None],
-        input_grad[None],
+        layer_out.T[None],
+        input_grad.T[None],
         qkv_sum,
-        out_sum[:query_width],
+        out_sum[:part_width].T,
         grad_gate,
         grad_up,
-        grad_down,
+        grad_down_t.T,
         grad_gain_attn,
-        out_sum[query_width],
+        grad_gain_mlp,
     )
 
 

time: 196 us -> 148 us (0.76)
  local copies, waits for them, and re-layouts: 43.7 us -> 8.16 us
  other arithmetic: 16 us -> 6.97 us
  waiting for transfers between devices: 23 us -> 19.4 us
    unnamed x55 -> x46, local copies, waits for them, and re-layouts: 17.9 us -> 3.17 us
    ppermute x6 -> x0, local copies, waits for them, and re-layouts: 14.2 us -> none  [swap(): return lax.ppermute(value, axis, [(i, i ^ distance) for i in range(count)])]
    concatenate x4 -> x0, other arithmetic: 4.65 us -> none  [the longest x2 2.49 us: whole_device(): jnp.concatenate([row_blocks, across_ctx(row_blocks, distance)], axis=0)]
    ppermute x19 -> x22, waiting for transfers between devices: 23 us -> 19.4 us  [swap(): return lax.ppermute(value, axis, [(i, i ^ distance) for i in range(count)])]
    optimization_barrier x1 -> x0, local copies, waits for them, and re-layouts: 3.52 us -> none  [whole_device(): mlp_half, low, high = lax.optimization_barrier((half_of(mlp, 1), low, high))]
    slice x4 -> x1, local copies, waits for them, and re-layouts: 2.55 us -> 0.01 us  [whole_device(): out_sum[part_width]]
    pallas_call x1 -> x0, local copies, waits for them, and re-layouts: 2.23 us -> none  [whole_device(): pl.pallas_call(own_mlp_kernel, in_specs=[SMEM] + [VMEM] * 5, out_specs=[V...]
    concatenate x2, other arithmetic: 2.27 us -> 0.09 us  [whole_device(): cot = jnp.concatenate([cot, across_ctx(cot, distance)], axis=0)]
  transfers between devices with their start and end apart: 19 -> 22, of which waited for: 8 -> 5; matrix products, arithmetic and copies ran while one was open for 27% -> 7% of each run, Pallas kernels for 46% -> 60%
where the time goes in v2:
time: 148 us
  Pallas kernels  89.2 us (60%)
  starting transfers between devices  23 us (16%)
  waiting for transfers between devices  19.4 us (13%)
  local copies, waits for them, and re-layouts  8.16 us (6%)
  other arithmetic  6.97 us (5%)
    pallas_call x1, Pallas kernels, whole_device(): pl.pallas_call(backward_kernel, in_specs=[VMEM] * 12, out_specs=[VMEM] *...  26.8 us
    ppermute x22, starting transfers between devices, swap(): return lax.ppermute(value, axis, [(i, i ^ distance) for i in range(count)])  23 us
    pallas_call x1, Pallas kernels, whole_device(): pl.pallas_call(forward_kernel, in_specs=[SMEM] + [VMEM] * 18, out_specs=[...  22.1 us
    ppermute x22, waiting for transfers between devices, swap(): return lax.ppermute(value, axis, [(i, i ^ distance) for i in range(count)])  19.4 us
    pallas_call x1, Pallas kernels, whole_device(): pl.pallas_call(other_mlp_kernel, in_specs=[SMEM] + [VMEM] * 10, out_specs...  18.1 us
    pallas_call x1, Pallas kernels, whole_device(): pl.pallas_call(own_mlp_kernel, in_specs=[SMEM] + [VMEM] * 7, out_specs=[V...  16.6 us
    pallas_call x1, Pallas kernels, whole_device(): pl.pallas_call(input_kernel, in_specs=[SMEM] + [VMEM] * 6, out_specs=VMEM...  5.63 us
    dynamic_slice x2, local copies, waits for them, and re-layouts, half_of(): return lax.dynamic_slice_in_dim(value, seq_index * half, half, axis)  3.3 us
  transfers between devices with their start and end apart: 22, of which 5 were waited for; matrix products, arithmetic and copies ran while one was open for 7% of the time, Pallas kernels for 60%

profile of v2, /device:TPU:0, one launch (start us, length us, event | category | flops | bytes accessed | tf_op | source)
XLA Modules:
  0.0 147.7 jit_solution(187229374347930543)
XLA Ops:
  0.7 3.1 %collective-permute-start.13 = (bf16[288,128]{1,0:T(8,128)(2,1)}, bf16[288,128]{1,0:T(8,128)(2,1)S(1)}, u32[]{:S(2)}, u32[]{:S(2)}) collective-permute-start(bf16[288,128]{1,0:T(8,128)(2,1)} %bitcast.41), channel_id=1, source_target_pairs={{0,1},{1,0},{2,3},{3,2},{4,5},{5,4},{6,7},{7,6},{8,9},{9,8},{10,11... | collective-permute-start | bytes 221192 | tf_op jit(solution)/shard_map/ppermute | solution.py:360
  3.7 2.6 %collective-permute-start = (bf16[288,128]{1,0:T(8,128)(2,1)}, bf16[288,128]{1,0:T(8,128)(2,1)}, u32[]{:S(2)}, u32[]{:S(2)}) collective-permute-start(bf16[288,128]{1,0:T(8,128)(2,1)} %bitcast.43), channel_id=1, source_target_pairs={{0,8},{2,10},{4,12},{6,14},{8,0},{10,2},{12,4},{14,6},{1,9},{3,11}... | collective-permute-start | bytes 221192 | tf_op jit(solution)/shard_map/ppermute | solution.py:360
  6.3 0.9 maximum_bitcast_fusion
  7.2 2.0 %collective-permute-start.14 = (bf16[1,2,288,128]{3,2,1,0:T(8,128)(2,1)S(1)}, bf16[1,2,288,128]{3,2,1,0:T(8,128)(2,1)S(1)}, u32[]{:S(2)}, u32[]{:S(2)}) collective-permute-start(bf16[1,2,288,128]{3,2,1,0:T(8,128)(2,1)S(1)} %maximum_bitcast_fusion), channel_id=1, source_target_pairs={{0,2},{2,0},{4,6},{6,4},{8,10},{10,8},{12,14},{14,12},{1,3},{3,1},... | collective-permute-start | bytes 442376 | tf_op jit(solution)/shard_map/ppermute | solution.py:360
  9.2 1.7 %constant_dynamic-slice_fusion = bf16[144,960]{1,0:T(8,128)(2,1)} fusion(bf16[288,960]{1,0:T(8,128)(2,1)} %proj_ref.1, s32[]{:T(128)S(6)} %select_n.13), kind=kLoop, calls=%fused_computation.18 | loop fusion | bytes 552964 | tf_op jit(solution)/shard_map/dynamic_slice | solution.py:789
  10.9 1.5 %collective-permute-start.8 = (bf16[144,960]{1,0:T(8,128)(2,1)}, bf16[144,960]{1,0:T(8,128)(2,1)S(1)}, u32[]{:S(2)}, u32[]{:S(2)}) collective-permute-start(bf16[144,960]{1,0:T(8,128)(2,1)} %constant_dynamic-slice_fusion), channel_id=1, source_target_pairs={{0,1},{1,0},{2,3},{3,2},{4,5},{5,4},{6,7},{7,6},{8,9},{9,8},{10,11... | collective-permute-start | bytes 829448 | tf_op jit(solution)/shard_map/ppermute | solution.py:360
  12.5 1.6 %dynamic-slice_bitcast_fusion.3 = bf16[144,576]{1,0:T(8,128)(2,1)} fusion(bf16[576,288]{0,1:T(8,128)(2,1)} %param.12, s32[]{:T(128)S(6)} %select_n.13), kind=kLoop, calls=%fused_computation.10 | loop fusion | bytes 331780 | tf_op jit(solution)/shard_map/dynamic_slice | solution.py:789
  14.1 0.5 collective-permute-start.10
  14.6 1.6 %collective-permute-start.15 = (bf16[2,2,288,128]{3,2,1,0:T(8,128)(2,1)S(1)}, bf16[2,2,288,128]{3,2,1,0:T(8,128)(2,1)S(1)}, u32[]{:S(2)}, u32[]{:S(2)}) collective-permute-start(bf16[2,2,288,128]{3,2,1,0:T(8,128)(2,1)S(1)} %pad_maximum_fusion.2), channel_id=1, source_target_pairs={{0,4},{2,6},{4,0},{6,2},{8,12},{10,14},{12,8},{14,10},{1,5},{3,7},... | collective-permute-start | bytes 884744 | tf_op jit(solution)/shard_map/ppermute | solution.py:360
  16.3 0.9 pad_maximum_fusion.3.one_ref
  17.2 0.5 collective-permute-start.1
  17.7 0.2 collective-permute-start.2
  18.0 0.1 dynamic-slice_bitcast_fusion.1
  18.0 6.8 %collective-permute-done.1.two_ref = bf16[2,288,128]{2,1,0:T(8,128)(2,1)} collective-permute-done((bf16[2,288,128]{2,1,0:T(8,128)(2,1)S(1)}, bf16[2,288,128]{2,1,0:T(8,128)(2,1)}, u32[]{:S(2)}, u32[]{:S(2)}) %collective-permute-start.1) | collective-permute-done | bytes 147488 | tf_op jit(solution)/shard_map/ppermute | solution.py:360
  24.8 1.4 collective-permute-start.5
  26.2 0.6 collective-permute-start.6
  26.9 0.1 pad_maximum_fusion.1.pairs_ref
  26.9 2.5 %collective-permute-start.16 = (bf16[4,2,288,128]{3,2,1,0:T(8,128)(2,1)S(1)}, bf16[4,2,288,128]{3,2,1,0:T(8,128)(2,1)S(1)}, u32[]{:S(2)}, u32[]{:S(2)}) collective-permute-start(bf16[4,2,288,128]{3,2,1,0:T(8,128)(2,1)S(1)} %pad_maximum_fusion.1.pairs_ref), channel_id=1, source_target_pairs={{0,8},{2,10},{4,12},{6,14},{8,0},{10,2},{12,4},{14,6},{1,9},{3,11}... | collective-permute-start | bytes 1769480 | tf_op jit(solution)/shard_map/ppermute | solution.py:360
  29.5 1.2 pad_maximum_fusion
  30.7 1.6 %collective-permute-start.4 = (bf16[2,288,128]{2,1,0:T(8,128)(2,1)S(1)}, bf16[2,288,128]{2,1,0:T(8,128)(2,1)S(1)}, u32[]{:S(2)}, u32[]{:S(2)}) collective-permute-start(bf16[2,288,128]{2,1,0:T(8,128)(2,1)S(1)} %pad_maximum_fusion.3.one_ref), channel_id=1, source_target_pairs={{0,1},{1,0},{2,3},{3,2},{4,5},{5,4},{6,7},{7,6},{8,9},{9,8},{10,11... | collective-permute-start | bytes 442376 | tf_op jit(solution)/shard_map/ppermute | solution.py:360
  32.3 0.7 collective-permute-start.7
  33.0 0.3 collective-permute-done.6.low_ref
  33.4 1.4 collective-permute-start.12
  34.8 2.7 %collective-permute-done.7.high_ref = bf16[2,288,128]{2,1,0:T(8,128)(2,1)S(1)} collective-permute-done((bf16[2,288,128]{2,1,0:T(8,128)(2,1)S(1)}, bf16[2,288,128]{2,1,0:T(8,128)(2,1)S(1)}, u32[]{:S(2)}, u32[]{:S(2)}) %collective-permute-start.7) | collective-permute-done | bytes 147488 | tf_op jit(solution)/shard_map/ppermute | solution.py:360
  37.5 0.8 collective-permute-start.3
  38.3 0.2 collective-permute-start.9
  38.4 0.8 collective-permute-start.17
  39.2 1.2 fusion
  40.4 0.7 pad_add_fusion.where_ref
  41.1 2.9 %collective-permute-done.3.near_two_ref = bf16[2,288,128]{2,1,0:T(8,128)(2,1)S(1)} collective-permute-done((bf16[2,288,128]{2,1,0:T(8,128)(2,1)}, bf16[2,288,128]{2,1,0:T(8,128)(2,1)S(1)}, u32[]{:S(2)}, u32[]{:S(2)}) %collective-permute-start.3) | collective-permute-done | bytes 147488 | tf_op jit(solution)/shard_map/ppermute | solution.py:360
  44.0 0.6 copy-done.18
  44.6 0.1 copy-done.11
  44.7 22.1 %forward.1 = (bf16[1024,576]{1,0:T(8,128)(2,1)}, bf16[288,1024]{1,0:T(8,128)(2,1)}, bf16[576,1024]{1,0:T(8,128)(2,1)}, bf16[192,1024]{1,0:T(8,128)(2,1)}, bf16[1...) custom-call(s32[3]{0:T(128)} %pad_add_fusion.where_ref, ...), custom_call_target="tpu_custom_call" | custom-call | tf_op jit(solution)/shard_map/forward/pallas_call | solution.py:823
  66.9 0.8 copy-done.6
  67.7 16.6 %own_mlp.1 = (bf16[1024,576]{1,0:T(8,128)(2,1)}, bf16[3,576,768]{2,1,0:T(8,128)(2,1)}, f32[1024,576]{1,0:T(8,128)}, f32[128,576]{1,0:T(8,128)}) custom-call(s32[3]{0:T(128)} %pad_add_fusion.where_ref, bf16[4,2,288,128]{3,2,1,0:T(8,128)(2,1)} %copy-done.2, bf16[4,2,288,128]{3,2,1,0:T(8,128)(2,1)} %copy-done.6, bf16[1024,576]{1,0:T(8,128)(2,1)} %get-tuple-element.38.h2_ref, ...), custom_call_target="tpu_custom_call" | custom-call | tf_op jit(solution)/shard_map/own_mlp/pallas_call | solution.py:852
  84.4 0.5 collective-permute-start.18
  84.9 6.7 %collective-permute-done.18.second_ref = bf16[3,288,768]{2,1,0:T(8,128)(2,1)} collective-permute-done((bf16[3,288,768]{2,1,0:T(8,128)(2,1)}, bf16[3,288,768]{2,1,0:T(8,128)(2,1)}, u32[]{:S(2)}, u32[]{:S(2)}) %collective-permute-start.18) | collective-permute-done | bytes 1327136 | tf_op jit(solution)/shard_map/ppermute | solution.py:360
  91.6 18.1 %other_mlp.1 = (bf16[288,128]{1,0:T(8,128)(2,1)}, f32[1024,576]{1,0:T(8,128)}, bf16[1024,576]{1,0:T(8,128)(2,1)}, bf16[304,576]{1,0:T(8,128)(2,1)}) custom-call(s32[3]{0:T(128)} %pad_add_fusion.where_ref, bf16[1024,576]{1,0:T(8,128)(2,1)} %get-tuple-element.38.h2_ref, bf16[1024,576]{1,0:T(8,128)(2,1)} %get-tuple-element.40.cot_ref, ...), custom_call_target="tpu_custom_call" | custom-call | tf_op jit(solution)/shard_map/other_mlp/pallas_call | solution.py:870
  109.6 0.1 collective-permute-start.21
  109.8 1.5 %copy-done.1 = bf16[3,576,768]{2,1,0:T(8,128)(2,1)} copy-done((bf16[3,576,768]{2,1,0:T(8,128)(2,1)}, bf16[3,576,768]{2,1,0:T(8,128)(2,1)S(1)}, u32[]{:S(2)}) %copy-start.1) | copy-done | bytes 2654232
  111.3 26.8 %backward.1 = (bf16[960,1024]{1,0:T(8,128)(2,1)}, bf16[288,960]{1,0:T(8,128)(2,1)}, f32[576,768]{1,0:T(8,128)}, f32[576,768]{1,0:T(8,128)}, f32[576,768]{1,0:T(8,128)}) custom-call(bf16[1536,576]{1,0:T(8,128)(2,1)} %get-tuple-element.47.weights_ref, bf16[1024,576]{1,0:T(8,128)(2,1)} %get-tuple-element.48.mid_bf_ref, ...), custom_call_target="tpu_custom_call" | custom-call | tf_op jit(solution)/shard_map/backward/pallas_call | solution.py:890
  138.1 0.4 collective-permute-start.20
  138.5 0.1 convert_add_fusion.1
  138.6 0.7 dynamic-slice_reduce_fusion
  139.3 0.9 slice_bitcast_fusion
  140.2 5.6 %input_grad.1 = f32[288,128]{1,0:T(8,128)} custom-call(s32[3]{0:T(128)} %pad_add_fusion.where_ref, bf16[960,1024]{1,0:T(8,128)(2,1)} %get-tuple-element.55.proj_ref, bf16[1536,576]{1,0:T(8,128)(2,1)} %get-tuple-element.47.weights_ref, bf16[1024,576]{1,0:T(8,128)(2,1)} %get-tuple-element.56.x_ref, f32[1024,576]{1,0:T(8,128)} %get-tuple-element.57.mid_ref, ...), custom_call_target="tpu_custom_call" | custom-call | tf_op jit(solution)/shard_map/input_grad/pallas_call | solution.py:914
  145.9 1.2 multiply_reduce_fusion
  147.1 0.6 div.17
  (68 shorter events, 0.2 us)
Async XLA Ops:
  0.6 17.3 %copy-start.3 = (bf16[768,576]{0,1:T(8,128)(2,1)S(1)}, bf16[768,576]{0,1:T(8,128)(2,1)}, u32[]{:S(2)}) copy-start(bf16[768,576]{0,1:T(8,128)(2,1)} %param.15) | copy-start | bytes 2654212
  0.7 5.7 %collective-permute-start.13 = (bf16[288,128]{1,0:T(8,128)(2,1)}, bf16[288,128]{1,0:T(8,128)(2,1)S(1)}, u32[]{:S(2)}, u32[]{:S(2)}) collective-permute-start(bf16[288,128]{1,0:T(8,128)(2,1)} %bitcast.41), channel_id=1, source_target_pairs={{0,1},{1,0},{2,3},{3,2},{4,5},{5,4},{6,7},{7,6},{8,9},{9,8},{10,11... | collective-permute-start | bytes 221192 | tf_op jit(solution)/shard_map/ppermute | solution.py:360
  3.7 12.5 %collective-permute-start = (bf16[288,128]{1,0:T(8,128)(2,1)}, bf16[288,128]{1,0:T(8,128)(2,1)}, u32[]{:S(2)}, u32[]{:S(2)}) collective-permute-start(bf16[288,128]{1,0:T(8,128)(2,1)} %bitcast.43), channel_id=1, source_target_pairs={{0,8},{2,10},{4,12},{6,14},{8,0},{10,2},{12,4},{14,6},{1,9},{3,11}... | collective-permute-start | bytes 221192 | tf_op jit(solution)/shard_map/ppermute | solution.py:360
  7.2 10.7 %copy-start.4 = (bf16[576,768]{1,0:T(8,128)(2,1)S(1)}, bf16[576,768]{1,0:T(8,128)(2,1)}, u32[]{:S(2)}) copy-start(bf16[576,768]{1,0:T(8,128)(2,1)} %gate_ref.1) | copy-start | bytes 2654212
  7.2 10.7 %copy-start.5 = (bf16[576,768]{1,0:T(8,128)(2,1)S(1)}, bf16[576,768]{1,0:T(8,128)(2,1)}, u32[]{:S(2)}) copy-start(bf16[576,768]{1,0:T(8,128)(2,1)} %up_ref.1) | copy-start | bytes 2654212
  7.2 7.3 %collective-permute-start.14 = (bf16[1,2,288,128]{3,2,1,0:T(8,128)(2,1)S(1)}, bf16[1,2,288,128]{3,2,1,0:T(8,128)(2,1)S(1)}, u32[]{:S(2)}, u32[]{:S(2)}) collective-permute-start(bf16[1,2,288,128]{3,2,1,0:T(8,128)(2,1)S(1)} %maximum_bitcast_fusion), channel_id=1, source_target_pairs={{0,2},{2,0},{4,6},{6,4},{8,10},{10,8},{12,14},{14,12},{1,3},{3,1},... | collective-permute-start | bytes 442376 | tf_op jit(solution)/shard_map/ppermute | solution.py:360
  10.9 27.3 %collective-permute-start.8 = (bf16[144,960]{1,0:T(8,128)(2,1)}, bf16[144,960]{1,0:T(8,128)(2,1)S(1)}, u32[]{:S(2)}, u32[]{:S(2)}) collective-permute-start(bf16[144,960]{1,0:T(8,128)(2,1)} %constant_dynamic-slice_fusion), channel_id=1, source_target_pairs={{0,1},{1,0},{2,3},{3,2},{4,5},{5,4},{6,7},{7,6},{8,9},{9,8},{10,11... | collective-permute-start | bytes 829448 | tf_op jit(solution)/shard_map/ppermute | solution.py:360
  14.1 16.6 %collective-permute-start.10 = (bf16[144,576]{1,0:T(8,128)(2,1)}, bf16[144,576]{1,0:T(8,128)(2,1)}, u32[]{:S(2)}, u32[]{:S(2)}) collective-permute-start(bf16[144,576]{1,0:T(8,128)(2,1)} %dynamic-slice_bitcast_fusion.3), channel_id=1, source_target_pairs={{0,1},{1,0},{2,3},{3,2},{4,5},{5,4},{6,7},{7,6},{8,9},{9,8},{10,11... | collective-permute-start | bytes 497672 | tf_op jit(solution)/shard_map/ppermute | solution.py:360
  14.6 12.3 %collective-permute-start.15 = (bf16[2,2,288,128]{3,2,1,0:T(8,128)(2,1)S(1)}, bf16[2,2,288,128]{3,2,1,0:T(8,128)(2,1)S(1)}, u32[]{:S(2)}, u32[]{:S(2)}) collective-permute-start(bf16[2,2,288,128]{3,2,1,0:T(8,128)(2,1)S(1)} %pad_maximum_fusion.2), channel_id=1, source_target_pairs={{0,4},{2,6},{4,0},{6,2},{8,12},{10,14},{12,8},{14,10},{1,5},{3,7},... | collective-permute-start | bytes 884744 | tf_op jit(solution)/shard_map/ppermute | solution.py:360
  17.2 13.5 %copy-start.7 = (bf16[2,288,128]{2,1,0:T(8,128)(2,1)}, bf16[2,288,128]{2,1,0:T(8,128)(2,1)S(1)}, u32[]{:S(2)}) copy-start(bf16[2,288,128]{2,1,0:T(8,128)(2,1)S(1)} %pad_maximum_fusion.3.one_ref) | copy-start | bytes 442372
  17.2 7.6 %collective-permute-start.1 = (bf16[2,288,128]{2,1,0:T(8,128)(2,1)S(1)}, bf16[2,288,128]{2,1,0:T(8,128)(2,1)}, u32[]{:S(2)}, u32[]{:S(2)}) collective-permute-start(bf16[2,288,128]{2,1,0:T(8,128)(2,1)S(1)} %pad_maximum_fusion.3.one_ref), channel_id=1, source_target_pairs={{0,4},{2,6},{4,0},{6,2},{8,12},{10,14},{12,8},{14,10},{1,5},{3,7},... | collective-permute-start | bytes 442376 | tf_op jit(solution)/shard_map/ppermute | solution.py:360
  17.7 8.5 %collective-permute-start.2 = (bf16[2,288,128]{2,1,0:T(8,128)(2,1)S(1)}, bf16[2,288,128]{2,1,0:T(8,128)(2,1)S(1)}, u32[]{:S(2)}, u32[]{:S(2)}) collective-permute-start(bf16[2,288,128]{2,1,0:T(8,128)(2,1)S(1)} %pad_maximum_fusion.3.one_ref), channel_id=1, source_target_pairs={{0,2},{2,0},{4,6},{6,4},{8,10},{10,8},{12,14},{14,12},{1,3},{3,1},... | collective-permute-start | bytes 442376 | tf_op jit(solution)/shard_map/ppermute | solution.py:360
  24.8 7.5 %collective-permute-start.5 = (bf16[2,288,128]{2,1,0:T(8,128)(2,1)}, bf16[2,288,128]{2,1,0:T(8,128)(2,1)S(1)}, u32[]{:S(2)}, u32[]{:S(2)}) collective-permute-start(bf16[2,288,128]{2,1,0:T(8,128)(2,1)} %collective-permute-done.1.two_ref), channel_id=1, source_target_pairs={{0,1},{1,0},{2,3},{3,2},{4,5},{5,4},{6,7},{7,6},{8,9},{9,8},{10,11... | collective-permute-start | bytes 442376 | tf_op jit(solution)/shard_map/ppermute | solution.py:360
  26.2 4.5 %copy-start.13 = (bf16[2,288,128]{2,1,0:T(8,128)(2,1)}, bf16[2,288,128]{2,1,0:T(8,128)(2,1)S(1)}, u32[]{:S(2)}) copy-start(bf16[2,288,128]{2,1,0:T(8,128)(2,1)S(1)} %collective-permute-done.2.near_one_ref) | copy-start | bytes 442372
  26.2 7.2 %collective-permute-start.6 = (bf16[2,288,128]{2,1,0:T(8,128)(2,1)S(1)}, bf16[2,288,128]{2,1,0:T(8,128)(2,1)S(1)}, u32[]{:S(2)}, u32[]{:S(2)}) collective-permute-start(bf16[2,288,128]{2,1,0:T(8,128)(2,1)S(1)} %collective-permute-done.2.near_one_ref), channel_id=1, source_target_pairs={{0,1},{1,0},{2,3},{3,2},{4,5},{5,4},{6,7},{7,6},{8,9},{9,8},{10,11... | collective-permute-start | bytes 442376 | tf_op jit(solution)/shard_map/ppermute | solution.py:360
  26.9 3.7 %copy-start.2 = (bf16[4,2,288,128]{3,2,1,0:T(8,128)(2,1)}, bf16[4,2,288,128]{3,2,1,0:T(8,128)(2,1)S(1)}, u32[]{:S(2)}) copy-start(bf16[4,2,288,128]{3,2,1,0:T(8,128)(2,1)S(1)} %pad_maximum_fusion.1.pairs_ref) | copy-start | bytes 1769476
  26.9 39.9 %collective-permute-start.16 = (bf16[4,2,288,128]{3,2,1,0:T(8,128)(2,1)S(1)}, bf16[4,2,288,128]{3,2,1,0:T(8,128)(2,1)S(1)}, u32[]{:S(2)}, u32[]{:S(2)}) collective-permute-start(bf16[4,2,288,128]{3,2,1,0:T(8,128)(2,1)S(1)} %pad_maximum_fusion.1.pairs_ref), channel_id=1, source_target_pairs={{0,8},{2,10},{4,12},{6,14},{8,0},{10,2},{12,4},{14,6},{1,9},{3,11}... | collective-permute-start | bytes 1769480 | tf_op jit(solution)/shard_map/ppermute | solution.py:360
  29.5 1.2 copy-start.22
  29.5 1.2 copy-start.21
  30.7 7.7 %collective-permute-start.4 = (bf16[2,288,128]{2,1,0:T(8,128)(2,1)S(1)}, bf16[2,288,128]{2,1,0:T(8,128)(2,1)S(1)}, u32[]{:S(2)}, u32[]{:S(2)}) collective-permute-start(bf16[2,288,128]{2,1,0:T(8,128)(2,1)S(1)} %pad_maximum_fusion.3.one_ref), channel_id=1, source_target_pairs={{0,1},{1,0},{2,3},{3,2},{4,5},{5,4},{6,7},{7,6},{8,9},{9,8},{10,11... | collective-permute-start | bytes 442376 | tf_op jit(solution)/shard_map/ppermute | solution.py:360
  32.3 11.6 %copy-start.14 = (bf16[2,288,128]{2,1,0:T(8,128)(2,1)}, bf16[2,288,128]{2,1,0:T(8,128)(2,1)S(1)}, u32[]{:S(2)}) copy-start(bf16[2,288,128]{2,1,0:T(8,128)(2,1)S(1)} %collective-permute-done.5.across_two_ref) | copy-start | bytes 442372
  32.3 5.1 %collective-permute-start.7 = (bf16[2,288,128]{2,1,0:T(8,128)(2,1)S(1)}, bf16[2,288,128]{2,1,0:T(8,128)(2,1)S(1)}, u32[]{:S(2)}, u32[]{:S(2)}) collective-permute-start(bf16[2,288,128]{2,1,0:T(8,128)(2,1)S(1)} %collective-permute-done.5.across_two_ref), channel_id=1, source_target_pairs={{0,2},{2,0},{4,6},{6,4},{8,10},{10,8},{12,14},{14,12},{1,3},{3,1},... | collective-permute-start | bytes 442376 | tf_op jit(solution)/shard_map/ppermute | solution.py:360
  33.0 10.9 %copy-start.19 = (f32[2,288]{1,0:T(2,128)}, f32[2,288]{1,0:T(2,128)S(1)}, u32[]{:S(2)}) copy-start(f32[2,288]{1,0:T(2,128)S(1)} %pad_maximum_fusion.4.gain_ref) | copy-start | bytes 6916
  33.4 10.6 %copy-start.15 = (bf16[2,288,128]{2,1,0:T(8,128)(2,1)}, bf16[2,288,128]{2,1,0:T(8,128)(2,1)S(1)}, u32[]{:S(2)}) copy-start(bf16[2,288,128]{2,1,0:T(8,128)(2,1)S(1)} %collective-permute-done.6.low_ref) | copy-start | bytes 442372
  33.4 4.1 %collective-permute-start.12 = (f32[2,288]{1,0:T(2,128)S(1)}, f32[2,288]{1,0:T(2,128)S(1)}, u32[]{:S(2)}, u32[]{:S(2)}) collective-permute-start(f32[2,288]{1,0:T(2,128)S(1)} %pad_maximum_fusion.4.gain_ref), channel_id=1, source_target_pairs={{0,1},{1,0},{2,3},{3,2},{4,5},{5,4},{6,7},{7,6},{8,9},{9,8},{10,11... | collective-permute-start | bytes 6920 | tf_op jit(solution)/shard_map/ppermute | solution.py:360
  37.5 6.5 %copy-start.17 = (bf16[2,288,128]{2,1,0:T(8,128)(2,1)}, bf16[2,288,128]{2,1,0:T(8,128)(2,1)S(1)}, u32[]{:S(2)}) copy-start(bf16[2,288,128]{2,1,0:T(8,128)(2,1)S(1)} %collective-permute-done.7.high_ref) | copy-start | bytes 442372
  37.5 3.6 %collective-permute-start.11 = (bf16[144,576]{1,0:T(8,128)(2,1)}, bf16[144,576]{1,0:T(8,128)(2,1)S(1)}, u32[]{:S(2)}, u32[]{:S(2)}) collective-permute-start(bf16[144,576]{1,0:T(8,128)(2,1)} %collective-permute-done.10.out_first_ref), channel_id=1, source_target_pairs={{0,16},{16,0},{1,17},{17,1},{2,18},{18,2},{3,19},{19,3},{4,20},{20... | collective-permute-start | bytes 497672 | tf_op jit(solution)/shard_map/ppermute | solution.py:360
  37.5 6.5 %copy-start.20 = (f32[2,288]{1,0:T(2,128)}, f32[2,288]{1,0:T(2,128)S(1)}, u32[]{:S(2)}) copy-start(f32[2,288]{1,0:T(2,128)S(1)} %collective-permute-done.12.other_gain_ref) | copy-start | bytes 6916
  37.5 6.5 %collective-permute-start.3 = (bf16[2,288,128]{2,1,0:T(8,128)(2,1)}, bf16[2,288,128]{2,1,0:T(8,128)(2,1)S(1)}, u32[]{:S(2)}, u32[]{:S(2)}) collective-permute-start(bf16[2,288,128]{2,1,0:T(8,128)(2,1)} %collective-permute-done.1.two_ref), channel_id=1, source_target_pairs={{0,2},{2,0},{4,6},{6,4},{8,10},{10,8},{12,14},{14,12},{1,3},{3,1},... | collective-permute-start | bytes 442376 | tf_op jit(solution)/shard_map/ppermute | solution.py:360
  38.3 5.7 %copy-start.10 = (bf16[144,960]{1,0:T(8,128)(2,1)}, bf16[144,960]{1,0:T(8,128)(2,1)S(1)}, u32[]{:S(2)}) copy-start(bf16[144,960]{1,0:T(8,128)(2,1)S(1)} %collective-permute-done.8.first_ref) | copy-start | bytes 829444
  38.3 5.7 %collective-permute-start.9 = (bf16[144,960]{1,0:T(8,128)(2,1)S(1)}, bf16[144,960]{1,0:T(8,128)(2,1)S(1)}, u32[]{:S(2)}, u32[]{:S(2)}) collective-permute-start(bf16[144,960]{1,0:T(8,128)(2,1)S(1)} %collective-permute-done.8.first_ref), channel_id=1, source_target_pairs={{0,16},{16,0},{1,17},{17,1},{2,18},{18,2},{3,19},{19,3},{4,20},{20... | collective-permute-start | bytes 829448 | tf_op jit(solution)/shard_map/ppermute | solution.py:360
  38.4 5.6 %copy-start.16 = (bf16[2,288,128]{2,1,0:T(8,128)(2,1)}, bf16[2,288,128]{2,1,0:T(8,128)(2,1)S(1)}, u32[]{:S(2)}) copy-start(bf16[2,288,128]{2,1,0:T(8,128)(2,1)S(1)} %collective-permute-done.4.across_one_ref) | copy-start | bytes 442372
  38.4 45.9 %collective-permute-start.17 = (bf16[3,288,768]{2,1,0:T(8,128)(2,1)}, bf16[3,288,768]{2,1,0:T(8,128)(2,1)}, u32[]{:S(2)}, u32[]{:S(2)}) collective-permute-start(bf16[3,288,768]{2,1,0:T(8,128)(2,1)} %pad_maximum_fusion), channel_id=1, source_target_pairs={{0,1},{1,0},{2,3},{3,2},{4,5},{5,4},{6,7},{7,6},{8,9},{9,8},{10,11... | collective-permute-start | bytes 3981320 | tf_op jit(solution)/shard_map/ppermute | solution.py:360
  41.1 3.0 %copy-start.12 = (bf16[144,576]{1,0:T(8,128)(2,1)}, bf16[144,576]{1,0:T(8,128)(2,1)S(1)}, u32[]{:S(2)}) copy-start(bf16[144,576]{1,0:T(8,128)(2,1)S(1)} %collective-permute-done.11.out_second_ref) | copy-start | bytes 497668
  43.9 0.7 copy-start.18
  44.0 0.8 copy-start.11
  66.9 0.8 copy-start.6
  84.4 25.4 %collective-permute-start.19 = (bf16[3,576,768]{2,1,0:T(8,128)(2,1)}, bf16[3,576,768]{2,1,0:T(8,128)(2,1)S(1)}, u32[]{:S(2)}, u32[]{:S(2)}) collective-permute-start(bf16[3,576,768]{2,1,0:T(8,128)(2,1)} %get-tuple-element.54.own_ref), channel_id=1, source_target_pairs={{0,16},{16,0},{1,17},{17,1},{2,18},{18,2},{3,19},{19,3},{4,20},{20... | collective-permute-start | bytes 7962632 | tf_op jit(solution)/shard_map/ppermute | solution.py:360
  84.4 7.2 %collective-permute-start.18 = (bf16[3,288,768]{2,1,0:T(8,128)(2,1)}, bf16[3,288,768]{2,1,0:T(8,128)(2,1)}, u32[]{:S(2)}, u32[]{:S(2)}) collective-permute-start(bf16[3,288,768]{2,1,0:T(8,128)(2,1)} %collective-permute-done.17.first_ref), channel_id=1, source_target_pairs={{0,16},{16,0},{1,17},{17,1},{2,18},{18,2},{3,19},{19,3},{4,20},{20... | collective-permute-start | bytes 3981320 | tf_op jit(solution)/shard_map/ppermute | solution.py:360
  109.6 28.9 %collective-permute-start.21 = (bf16[304,576]{1,0:T(8,128)(2,1)}, bf16[304,576]{1,0:T(8,128)(2,1)S(1)}, u32[]{:S(2)}, u32[]{:S(2)}) collective-permute-start(bf16[304,576]{1,0:T(8,128)(2,1)} %get-tuple-element.59), channel_id=1, source_target_pairs={{0,16},{16,0},{1,17},{17,1},{2,18},{18,2},{3,19},{19,3},{4,20},{20... | collective-permute-start | bytes 1050632 | tf_op jit(solution)/shard_map/ppermute | solution.py:360
  109.8 1.5 %copy-start.1 = (bf16[3,576,768]{2,1,0:T(8,128)(2,1)}, bf16[3,576,768]{2,1,0:T(8,128)(2,1)S(1)}, u32[]{:S(2)}) copy-start(bf16[3,576,768]{2,1,0:T(8,128)(2,1)S(1)} %collective-permute-done.19.got_ref) | copy-start | bytes 7962628
  111.3 27.2 %copy-start.9 = (bf16[304,576]{1,0:T(8,128)(2,1)S(1)}, bf16[304,576]{1,0:T(8,128)(2,1)}, u32[]{:S(2)}) copy-start(bf16[304,576]{1,0:T(8,128)(2,1)} %get-tuple-element.59) | copy-start | bytes 1050628
  138.1 7.8 %collective-permute-start.20 = (bf16[288,960]{1,0:T(8,128)(2,1)}, bf16[288,960]{1,0:T(8,128)(2,1)S(1)}, u32[]{:S(2)}, u32[]{:S(2)}) collective-permute-start(bf16[288,960]{1,0:T(8,128)(2,1)} %get-tuple-element.58), channel_id=1, source_target_pairs={{0,16},{16,0},{1,17},{17,1},{2,18},{18,2},{3,19},{19,3},{4,20},{20... | collective-permute-start | bytes 1658888 | tf_op jit(solution)/shard_map/ppermute | solution.py:360
  140.2 5.6 %copy-start = (bf16[288,960]{1,0:T(8,128)(2,1)S(1)}, bf16[288,960]{1,0:T(8,128)(2,1)}, u32[]{:S(2)}) copy-start(bf16[288,960]{1,0:T(8,128)(2,1)} %proj_ref.1) | copy-start | bytes 1658884
  140.2 5.6 %copy-start.8 = (bf16[288,960]{1,0:T(8,128)(2,1)S(1)}, bf16[288,960]{1,0:T(8,128)(2,1)}, u32[]{:S(2)}) copy-start(bf16[288,960]{1,0:T(8,128)(2,1)} %get-tuple-element.58) | copy-start | bytes 1658884
